TPU v7x, 128 devices: a whole 4x4x4 slice. The times are simulated.
128 devices in a mesh: depth: 64 (over x_lo, y, z, core), filt: 2 (over x_hi).
Axes of the slice: x: 4 (x_hi: 2, x_lo: 2; x = x_hi * 2 + x_lo), y: 4, z: 4, core: 2. Of those that a mesh axis runs over, the one named last changes fastest.
Arguments:
- volume: bfloat16 [128, 64, 1024], P('filt', 'depth'), may hold values from -6 to 6
- up_weight: bfloat16 [128, 4096], P(None, 'filt'), may hold values from -0.1875 to 0.1875
- up_bias: float32 [64], P('filt'), may hold values from -3 to 3
- first_weight: bfloat16 [27, 4096], replicated, may hold values from -0.15625 to 0.15625
- first_bias: float32 [64], replicated, may hold values from -3 to 3
- second_weight: bfloat16 [27, 4096], replicated, may hold values from -0.15625 to 0.15625
- second_bias: float32 [64], replicated, may hold values from -3 to 3
Outputs:
- decoded: bfloat16 [64, 128, 32, 128], P('filt', 'depth')
All inputs are finite; a program needn't handle non-finite values.
Results may differ from a plain program's by a relative error of at most 0.0052.
Values may be sent and summed in bfloat16 or wider, within the bound.
No kernel may reach another device: no remote copies, remote signals or barrier semaphores. Data moves between devices by JAX's collectives and lax.ppermute only.
A program may use at most 64 MiB of HBM per device.

v0:
```python
import jax
import jax.numpy as jnp
from jax import lax
from jax.experimental import pallas as pl
from jax.experimental.pallas import tpu as pltpu
from jax.sharding import PartitionSpec as P


F32 = jnp.float32
BF16 = jnp.bfloat16
VMEM = pl.BlockSpec(memory_space=pltpu.VMEM)
SMEM = pl.BlockSpec(memory_space=pltpu.SMEM)
NT = (((1,), (1,)), ((), ()))


def params(mebibytes):
    return pltpu.CompilerParams(vmem_limit_bytes=mebibytes * 2**20)


def cost(flops, count):
    return pl.CostEstimate(flops=flops, bytes_accessed=count, transcendentals=0)


def lanes_of(shape):
    return lax.broadcasted_iota(jnp.int32, shape, len(shape) - 1)


def leaky(value):
    return jnp.where(value > 0, value, 0.2 * value)


def up_weight_kernel(weight_ref, bias_ref, own_ref, send_ref, rows):
    rows[...] = weight_ref[...].astype(F32).T
    for k in range(64):
        block = rows[pl.ds(k, 32, stride=64), :]
        own_ref[k // 32, pl.ds((k % 32) * 32, 32), :] = block.astype(BF16)
    bias = jnp.concatenate([bias_ref[...]] * 4, axis=1)
    high = bias.astype(BF16).astype(F32)
    middle = (bias - high).astype(BF16).astype(F32)
    low = bias - high - middle
    row = lax.broadcasted_iota(jnp.int32, (16, 128), 0)
    parts = jnp.where(row == 0, high, jnp.where(row == 1, middle, jnp.where(row == 2, low, 0.0)))
    for half in range(2):
        own_ref[half, pl.ds(1024, 16), :] = parts.astype(BF16)
    send_ref[...] = own_ref[lax.axis_index("depth") % 2]


def prepare_up(weight, bias_row):
    return pl.pallas_call(
        up_weight_kernel,
        out_shape=(jax.ShapeDtypeStruct((2, 1040, 128), BF16), jax.ShapeDtypeStruct((1040, 128), BF16)),
        in_specs=[VMEM, VMEM],
        out_specs=(VMEM, VMEM),
        scratch_shapes=[pltpu.VMEM((2048, 128), F32)],
        compiler_params=params(12),
        cost_estimate=cost(10**9, 2 * 2**20),
        name="prepare_up",
    )(weight, bias_row)


def conv_weight_kernel(first_ref, second_ref, one_ref, two_ref, spread):
    lane = lanes_of((1, 128))

    def arrange(source, start, count, out_ref):
        for pair in range(count // 2):
            chunk = source[:, pl.ds(start + pair * 128, 128)].astype(F32)
            spread[pl.ds(2 * pair, 27, stride=64), :] = chunk
            spread[pl.ds(2 * pair + 1, 27, stride=64), :] = pltpu.roll(chunk, 64, 1)
        for eh in range(3):
            for ew in range(3):
                for zp in range(2):
                    for zo in range(2):
                        halves = []
                        for zi in range(2):
                            ed = 2 * zp + zi - zo
                            if 0 <= ed < 3:
                                tap = spread[pl.ds((9 * ed + 3 * eh + ew) * 64, count), :]
                                halves.append(pltpu.roll(tap, 64, 1) if zi else tap)
                            else:
                                halves.append(jnp.zeros((count, 128), F32))
                        block = jnp.where(lane < 64, halves[0], halves[1])
                        row, column = (ew * 2 + zo) * count, (eh * 2 + zp) * 128
                        out_ref[pl.ds(row, count), pl.ds(column, 128)] = block.astype(BF16)

    arrange(first_ref, 0, 64, one_ref)
    arrange(second_ref, pl.multiple_of(lax.axis_index("filt") * 2048, 2048), 32, two_ref)


def prepare_convs(first, second):
    return pl.pallas_call(
        conv_weight_kernel,
        out_shape=(jax.ShapeDtypeStruct((384, 768), BF16), jax.ShapeDtypeStruct((192, 768), BF16)),
        in_specs=[VMEM, VMEM],
        out_specs=(VMEM, VMEM),
        scratch_shapes=[pltpu.VMEM((27 * 64, 128), F32)],
        compiler_params=params(12),
        cost_estimate=cost(10**9, 2 * 2**20),
        name="prepare_convs",
    )(first, second)


def main_kernel(
    own_ref, near_ref, far_ref, last_ref, up_own_ref, up_near_ref, up_far_ref,
    one_ref, two_ref, bias_one_ref, bias_two_ref,
    out_ref,
    cells, up_weight, natural, upsampled, taps, hidden, rows_out,
):
    depth = lax.axis_index("depth")
    filt = lax.axis_index("filt")
    odd = depth % 2
    not_first = (depth != 0).astype(F32)
    not_last = (depth != lax.axis_size("depth") - 1).astype(F32)
    lane = lanes_of((1, 128))

    def place_half(source, where_f, ks):
        for k in ks:
            kd, kh, kw = 3 - k // 16, 3 - (k // 4) % 4, k % 4
            zin, zz = kd // 2, kd % 2
            hk, a = kh // 2, kh % 2
            place = ((3, 0, 1, 2), (2, 1, 0, 3))[zz][kw]
            row = pl.multiple_of(64 * place + 32 * where_f, 32)
            up_weight[a, zz, pl.ds(row, 32), pl.ds((hk * 2 + zin) * 128, 128)] = source(k)

    def part(ref, k):
        return ref[pl.ds((k % 32) * 32, 32), :]

    is_even = odd == 0
    place_half(lambda k: part(up_own_ref.at[k // 32], k), filt, range(64))
    place_half(lambda k: jnp.where(is_even, part(up_near_ref, k), part(up_far_ref, k)), 1 - filt, range(32))
    place_half(lambda k: jnp.where(is_even, part(up_far_ref, k), part(up_near_ref, k)), 1 - filt, range(32, 64))

    def bias_of(block):
        parts = block.astype(F32)
        return parts[0:1] + parts[1:2] + parts[2:3]

    mine = bias_of(up_own_ref[0, pl.ds(1024, 16), :])
    theirs = bias_of(up_near_ref[pl.ds(1024, 16), :])
    is_low = filt == 0
    bias_up = jnp.where(
        (lane // 32) % 2 == 0, jnp.where(is_low, mine, theirs), jnp.where(is_low, theirs, mine)
    )

    def column_of(row):
        return jnp.broadcast_to(row, (128, 128)).T

    row = bias_one_ref[...]
    bias_one = column_of(jnp.concatenate([row, row], axis=1))
    row = bias_two_ref[...]
    row = jnp.where(is_low, row[:, 0:32], row[:, 32:64])
    bias_two = column_of(jnp.concatenate([row] * 4, axis=1))[0:64]

    for i in range(5):
        cells[i, 0:64, :] = jnp.zeros((64, 128), BF16)
        cells[i, 1088:1152, :] = jnp.zeros((64, 128), BF16)

    def place_plane(plane, index):
        cells[index, 64:1088, :] = plane.T

    place_plane(own_ref[...], 2)
    place_plane(near_ref[...], 3 - 2 * odd)
    place_plane(far_ref[0], 3 * odd)
    place_plane(far_ref[1], 1 + 3 * odd)
    place_plane(last_ref[...], 4 - 4 * odd)

    upsampled[0:128, :] = jnp.zeros((128, 384), BF16)
    upsampled[4224:4352, :] = jnp.zeros((128, 384), BF16)
    hidden[:, 0:128] = jnp.zeros((256, 128), BF16)
    hidden[:, 4224:4352] = jnp.zeros((256, 128), BF16)

    width = lax.broadcasted_iota(jnp.int32, (1024, 128), 0) % 64
    low_lanes = lanes_of((1024, 128)) < 64

    for i in range(3):
        keep = (not_first, None, not_last)[i]
        for a in range(2):
            planes = []
            for zz in range(2):
                pair = i + zz
                lhs = jnp.concatenate(
                    [cells[pair + zin, (a + hk) * 64 : (a + hk) * 64 + 1024, :] for hk in range(2) for zin in range(2)],
                    axis=1,
                )
                total = lax.dot_general(lhs, up_weight[a, zz], NT, preferred_element_type=F32)
                aside = total[:, 128:256]
                before = jnp.where(width == 0, 0.0, pltpu.roll(aside, 1, 0))
                after = jnp.where(width == 63, 0.0, pltpu.roll(aside, 1023, 0))
                even_first = low_lanes if zz == 0 else jnp.logical_not(low_lanes)
                value = total[:, 0:128] + jnp.where(even_first, before, after) + bias_up
                planes.append(value if keep is None else value * keep)
            even = jnp.where(low_lanes, planes[0], planes[1])
            uneven = pltpu.roll(jnp.where(low_lanes, planes[1], planes[0]), 64, 1)
            for h in range(16):
                for b, value in ((0, even), (1, uneven)):
                    natural[pl.ds((2 * h + a) * 128 + b, 64, stride=2), :] = value[h * 64 : h * 64 + 64]
        upsampled[128:4224, i * 128 : i * 128 + 128] = natural[...].astype(BF16)

    def combine(count, h):
        where = pl.ds(h * 128, 128)
        column = lanes_of((count, 128))
        value = taps[count : 2 * count, where]
        value = value + jnp.where(column == 0, 0.0, pltpu.roll(taps[0:count, where], 1, 1))
        return value + jnp.where(column == 127, 0.0, pltpu.roll(taps[2 * count : 3 * count, where], 127, 1))

    upper = lax.broadcasted_iota(jnp.int32, (128, 128), 0) < 64
    for g in range(2):
        rhs = jnp.concatenate(
            [upsampled[eh * 128 : eh * 128 + 4096, g * 128 : g * 128 + 256] for eh in range(3)], axis=1
        )
        taps[...] = lax.dot_general(one_ref[...], rhs, NT, preferred_element_type=F32)
        keep = jnp.where(upper, not_first, 1.0) if g == 0 else jnp.where(upper, 1.0, not_last)
        for h in range(32):
            value = leaky(combine(128, h) + bias_one) * keep
            hidden[g * 128 : g * 128 + 128, (h + 1) * 128 : (h + 2) * 128] = value.astype(BF16)

    rhs = jnp.concatenate([hidden[:, eh * 128 : eh * 128 + 4096] for eh in range(3)], axis=0)
    taps[0:192, :] = jnp.dot(two_ref[...], rhs, preferred_element_type=F32)
    for h in range(32):
        value = leaky(combine(64, h) + bias_two)
        for z in range(2):
            rows_out[pl.ds(z * 32 + h, 32, stride=64), :] = value[z * 32 : z * 32 + 32]
    out_ref[...] = rows_out[...].reshape(32, 2, 32, 128).astype(BF16)


def section(*operands):
    return pl.pallas_call(
        main_kernel,
        out_shape=jax.ShapeDtypeStruct((32, 2, 32, 128), BF16),
        in_specs=[VMEM] * 11,
        out_specs=VMEM,
        scratch_shapes=[
            pltpu.VMEM((5, 18 * 64, 128), BF16),
            pltpu.VMEM((2, 2, 256, 512), BF16),
            pltpu.VMEM((4096, 128), F32),
            pltpu.VMEM((34 * 128, 384), BF16),
            pltpu.VMEM((384, 4096), F32),
            pltpu.VMEM((256, 34 * 128), BF16),
            pltpu.VMEM((2048, 128), F32),
        ],
        compiler_params=params(40),
        cost_estimate=cost(10**10, 6 * 2**20),
        name="section",
    )(*operands)


def shards(volume, up_weight, up_bias, first_weight, first_bias, second_weight, second_bias):
    devices = lax.axis_size("depth")
    odd = lax.axis_index("depth") % 2
    filt = lax.axis_index("filt")
    swap = [(0, 1), (1, 0)]
    siblings = [(i, i ^ 1) for i in range(devices)]
    across = [(i, i + 1) for i in range(1, devices - 1, 2)]
    across = across + [(j, i) for i, j in across]

    other = lax.ppermute(volume, "filt", swap)
    up_own, up_send = prepare_up(up_weight, up_bias[None])
    up_near = lax.ppermute(up_send, "filt", swap)
    up_far = lax.ppermute(up_near, "depth", siblings)
    one, two = prepare_convs(first_weight, second_weight)
    mine = volume.reshape(64, 1024)
    theirs = other.reshape(64, 1024)
    own = jnp.where(filt == 0, jnp.concatenate([mine, theirs]), jnp.concatenate([theirs, mine]))
    near = lax.ppermute(own, "depth", siblings)
    both = jnp.where(odd == 0, jnp.stack([own, near]), jnp.stack([near, own]))
    far = lax.ppermute(both, "depth", across)
    relay = lax.dynamic_index_in_dim(far, 1 - odd, 0, keepdims=False)
    last = lax.ppermute(relay, "depth", siblings)
    return section(
        own, near, far, last, up_own, up_near, up_far, one, two, first_bias[None], second_bias[None]
    )


def solution(mesh):
    placed = (P("filt", "depth", None), P(None, "filt"), P("filt"), P(), P(), P(), P())
    return jax.shard_map(
        shards,
        mesh=mesh,
        in_specs=placed,
        out_specs=P("filt", "depth", None, None),
        check_vma=False,
    )
```

profile of v0, /device:TPU:2, one launch (start us, length us, event | category | flops | bytes accessed | tf_op | source)
XLA Modules:
  0.0 46.2 jit_solution(17304825710639193856)
XLA Ops:
  0.0 2.1 %collective-permute-start = (bf16[64,1,1024]{2,0,1:T(8,128)(2,1)}, bf16[64,1,1024]{2,0,1:T(8,128)(2,1)S(1)}, u32[]{:S(2)}, u32[]{:S(2)}) collective-permute-start(bf16[64,1,1024]{2,0,1:T(8,128)(2,1)} %param.7), channel_id=1, source_target_pairs={{0,1},{1,0},{2,3},{3,2},{4,5},{5,4},{6,7},{7,6},{8,9},{9,8},{10,11... | collective-permute-start | bytes 393224 | tf_op jit(solution)/shard_map/ppermute | solution.py:254
  2.1 4.8 %collective-permute-done = bf16[64,1,1024]{2,0,1:T(8,128)(2,1)S(1)} collective-permute-done((bf16[64,1,1024]{2,0,1:T(8,128)(2,1)}, bf16[64,1,1024]{2,0,1:T(8,128)(2,1)S(1)}, u32[]{:S(2)}, u32[]{:S(2)}) %collective-permute-start) | collective-permute-done | bytes 131104 | tf_op jit(solution)/shard_map/ppermute | solution.py:254
  7.0 0.0 copy-start.6
  7.0 1.1 %maximum_select_fusion.1.own_ref = bf16[128,1024]{1,0:T(8,128)(2,1)S(1)} fusion(bf16[64,1024]{1,0:T(8,128)(2,1)S(1)} %bitcast.16, bf16[64,1024]{1,0:T(8,128)(2,1)} %bitcast.14, pred[]{:T(512)S(6)} %eq.8), kind=kLoop, calls=%fused_computation.1 | loop fusion | flops 1179648 | bytes 524289 | tf_op jit(solution)/shard_map/jit(_where)/select_n | solution.py:261
  8.1 0.1 collective-permute-start.1
  8.2 0.0 copy-done.6
  8.2 0.1 maximum_select_fusion.2
  8.2 1.4 %collective-permute-done.1.near_ref = bf16[128,1024]{1,0:T(8,128)(2,1)S(1)} collective-permute-done((bf16[128,1024]{1,0:T(8,128)(2,1)S(1)}, bf16[128,1024]{1,0:T(8,128)(2,1)S(1)}, u32[]{:S(2)}, u32[]{:S(2)}) %collective-permute-start.1) | collective-permute-done | bytes 262176 | tf_op jit(solution)/shard_map/ppermute | solution.py:262
  9.7 0.0 copy-start
  9.7 0.1 maximum_select_fusion
  9.8 0.0 copy-start.3
  9.8 8.2 %collective-permute-start.2 = (bf16[2,128,1024]{2,1,0:T(8,128)(2,1)S(1)}, bf16[2,128,1024]{2,1,0:T(8,128)(2,1)S(1)}, u32[]{:S(2)}, u32[]{:S(2)}) collective-permute-start(bf16[2,128,1024]{2,1,0:T(8,128)(2,1)S(1)} %maximum_select_fusion), channel_id=1, source_target_pairs={{2,4},{6,8},{10,12},{14,16},{18,20},{22,24},{26,28},{30,32},{34,36... | collective-permute-start | bytes 1572872 | tf_op jit(solution)/shard_map/ppermute | solution.py:264
  18.0 0.0 copy-done
  18.0 0.0 copy-done.3
  18.0 0.8 %prepare_up.1 = (bf16[2,1040,128]{2,1,0:T(8,128)(2,1)S(1)}, bf16[1040,128]{1,0:T(8,128)(2,1)S(1)}) custom-call(bf16[128,2048]{1,0:T(8,128)(2,1)S(1)} %copy-done, f32[1,32]{1,0:T(1,128)S(1)} %bitcast.11), custom_call_target="tpu_custom_call" | custom-call | flops 1000000000 | bytes 2097152 | tf_op jit(solution)/shard_map/prepare_up/pallas_call | solution.py:49
  18.9 2.5 %collective-permute-start.4 = (bf16[1040,128]{1,0:T(8,128)(2,1)S(1)}, bf16[1040,128]{1,0:T(8,128)(2,1)S(1)}, u32[]{:S(2)}, u32[]{:S(2)}) collective-permute-start(bf16[1040,128]{1,0:T(8,128)(2,1)S(1)} %get-tuple-element.10), channel_id=1, source_target_pairs={{0,1},{1,0},{2,3},{3,2},{4,5},{5,4},{6,7},{7,6},{8,9},{9,8},{10,11... | collective-permute-start | bytes 798728 | tf_op jit(solution)/shard_map/ppermute | solution.py:256
  21.4 0.0 copy-start.1
  21.4 0.0 copy-start.2
  21.4 9.1 %collective-permute-done.4.up_near_ref = bf16[1040,128]{1,0:T(8,128)(2,1)S(1)} collective-permute-done((bf16[1040,128]{1,0:T(8,128)(2,1)S(1)}, bf16[1040,128]{1,0:T(8,128)(2,1)S(1)}, u32[]{:S(2)}, u32[]{:S(2)}) %collective-permute-start.4) | collective-permute-done | bytes 266272 | tf_op jit(solution)/shard_map/ppermute | solution.py:256
  30.4 0.0 collective-permute-start.5
  30.4 0.0 collective-permute-done.2.far_ref
  30.5 0.8 %collective-permute-start.3 = (bf16[128,1024]{1,0:T(8,128)(2,1)S(1)}, bf16[128,1024]{1,0:T(8,128)(2,1)S(1)}, u32[]{:S(2)}, u32[]{:S(2)}) collective-permute-start(bf16[128,1024]{1,0:T(8,128)(2,1)S(1)} %dynamic-slice_bitcast_fusion), channel_id=1, source_target_pairs={{0,2},{2,0},{4,6},{6,4},{8,10},{10,8},{12,14},{14,12},{16,18},{18,... | collective-permute-start | bytes 786440 | tf_op jit(solution)/shard_map/ppermute | solution.py:266
  31.2 0.0 copy-done.1
  31.2 0.0 copy-done.2
  31.2 1.5 %prepare_convs.1 = (bf16[384,768]{1,0:T(8,128)(2,1)S(1)}, bf16[192,768]{1,0:T(8,128)(2,1)S(1)}) custom-call(bf16[27,4096]{1,0:T(8,128)(2,1)S(1)} %copy-done.1, bf16[27,4096]{1,0:T(8,128)(2,1)S(1)} %copy-done.2), custom_call_target="tpu_custom_call" | custom-call | flops 1000000000 | bytes 2097152 | tf_op jit(solution)/shard_map/prepare_convs/pallas_call | solution.py:90
  32.7 0.0 collective-permute-done.5.up_far_ref
  32.7 0.0 collective-permute-done.3.last_ref
  32.7 0.0 copy-start.4
  32.7 0.0 copy-start.5
  32.8 0.6 %copy-done.4 = f32[64]{0:T(128)S(1)} copy-done((f32[64]{0:T(128)S(1)}, f32[64]{0:T(128)}, u32[]{:S(2)}) %copy-start.4) | copy-done | bytes 280
  33.4 0.0 copy-done.5
  33.4 12.8 %section.1 = bf16[32,2,32,128]{3,2,1,0:T(8,128)(2,1)} custom-call(bf16[128,1024]{1,0:T(8,128)(2,1)S(1)} %maximum_select_fusion.1.own_ref, bf16[128,1024]{1,0:T(8,128)(2,1)S(1)} %collective-permute-done.1.near_ref, bf16[2,128,1024]{2,1,0:T(8,128)(2,1)S(1)} %collective-permute-done.2.far_ref, bf16[128,1024]{1,0:T(8,128)(2,1)S(1)} %collective-permute-done.3.last_ref, ...), custom_call_target="tpu_custom_call" | custom-call | flops 10000000000 | bytes 6291456 | tf_op jit(solution)/shard_map/section/pallas_call | solution.py:225
  (1 shorter events, 0.0 us)
Async XLA Ops:
  0.0 7.0 %collective-permute-start = (bf16[64,1,1024]{2,0,1:T(8,128)(2,1)}, bf16[64,1,1024]{2,0,1:T(8,128)(2,1)S(1)}, u32[]{:S(2)}, u32[]{:S(2)}) collective-permute-start(bf16[64,1,1024]{2,0,1:T(8,128)(2,1)} %param.7), channel_id=1, source_target_pairs={{0,1},{1,0},{2,3},{3,2},{4,5},{5,4},{6,7},{7,6},{8,9},{9,8},{10,11... | collective-permute-start | bytes 393224 | tf_op jit(solution)/shard_map/ppermute | solution.py:254
  7.0 1.2 %copy-start.6 = (bf16[64,1,1024]{2,0,1:T(8,128)(2,1)S(1)}, bf16[64,1,1024]{2,0,1:T(8,128)(2,1)}, u32[]{:S(2)}) copy-start(bf16[64,1,1024]{2,0,1:T(8,128)(2,1)} %param.7) | copy-start | bytes 393220
  8.1 1.6 %collective-permute-start.1 = (bf16[128,1024]{1,0:T(8,128)(2,1)S(1)}, bf16[128,1024]{1,0:T(8,128)(2,1)S(1)}, u32[]{:S(2)}, u32[]{:S(2)}) collective-permute-start(bf16[128,1024]{1,0:T(8,128)(2,1)S(1)} %maximum_select_fusion.1.own_ref), channel_id=1, source_target_pairs={{0,2},{2,0},{4,6},{6,4},{8,10},{10,8},{12,14},{14,12},{16,18},{18,... | collective-permute-start | bytes 786440 | tf_op jit(solution)/shard_map/ppermute | solution.py:262
  9.7 8.3 %copy-start = (bf16[128,2048]{1,0:T(8,128)(2,1)S(1)}, bf16[128,2048]{1,0:T(8,128)(2,1)}, u32[]{:S(2)}) copy-start(bf16[128,2048]{1,0:T(8,128)(2,1)} %weight_ref.1) | copy-start | bytes 1572868
  9.8 8.3 %copy-start.3 = (f32[32]{0:T(128)S(1)}, f32[32]{0:T(128)}, u32[]{:S(2)}) copy-start(f32[32]{0:T(128)} %param.9) | copy-start | bytes 388
  9.8 20.7 %collective-permute-start.2 = (bf16[2,128,1024]{2,1,0:T(8,128)(2,1)S(1)}, bf16[2,128,1024]{2,1,0:T(8,128)(2,1)S(1)}, u32[]{:S(2)}, u32[]{:S(2)}) collective-permute-start(bf16[2,128,1024]{2,1,0:T(8,128)(2,1)S(1)} %maximum_select_fusion), channel_id=1, source_target_pairs={{2,4},{6,8},{10,12},{14,16},{18,20},{22,24},{26,28},{30,32},{34,36... | collective-permute-start | bytes 1572872 | tf_op jit(solution)/shard_map/ppermute | solution.py:264
  18.9 11.6 %collective-permute-start.4 = (bf16[1040,128]{1,0:T(8,128)(2,1)S(1)}, bf16[1040,128]{1,0:T(8,128)(2,1)S(1)}, u32[]{:S(2)}, u32[]{:S(2)}) collective-permute-start(bf16[1040,128]{1,0:T(8,128)(2,1)S(1)} %get-tuple-element.10), channel_id=1, source_target_pairs={{0,1},{1,0},{2,3},{3,2},{4,5},{5,4},{6,7},{7,6},{8,9},{9,8},{10,11... | collective-permute-start | bytes 798728 | tf_op jit(solution)/shard_map/ppermute | solution.py:256
  21.4 9.9 %copy-start.1 = (bf16[27,4096]{1,0:T(8,128)(2,1)S(1)}, bf16[27,4096]{1,0:T(8,128)(2,1)}, u32[]{:S(2)}) copy-start(bf16[27,4096]{1,0:T(8,128)(2,1)} %first_ref.1) | copy-start | bytes 663556
  21.4 9.9 %copy-start.2 = (bf16[27,4096]{1,0:T(8,128)(2,1)S(1)}, bf16[27,4096]{1,0:T(8,128)(2,1)}, u32[]{:S(2)}) copy-start(bf16[27,4096]{1,0:T(8,128)(2,1)} %second_ref.1) | copy-start | bytes 663556
  30.4 2.3 %collective-permute-start.5 = (bf16[1040,128]{1,0:T(8,128)(2,1)S(1)}, bf16[1040,128]{1,0:T(8,128)(2,1)S(1)}, u32[]{:S(2)}, u32[]{:S(2)}) collective-permute-start(bf16[1040,128]{1,0:T(8,128)(2,1)S(1)} %collective-permute-done.4.up_near_ref), channel_id=1, source_target_pairs={{0,2},{2,0},{4,6},{6,4},{8,10},{10,8},{12,14},{14,12},{16,18},{18,... | collective-permute-start | bytes 798728 | tf_op jit(solution)/shard_map/ppermute | solution.py:257
  30.5 2.3 %collective-permute-start.3 = (bf16[128,1024]{1,0:T(8,128)(2,1)S(1)}, bf16[128,1024]{1,0:T(8,128)(2,1)S(1)}, u32[]{:S(2)}, u32[]{:S(2)}) collective-permute-start(bf16[128,1024]{1,0:T(8,128)(2,1)S(1)} %dynamic-slice_bitcast_fusion), channel_id=1, source_target_pairs={{0,2},{2,0},{4,6},{6,4},{8,10},{10,8},{12,14},{14,12},{16,18},{18,... | collective-permute-start | bytes 786440 | tf_op jit(solution)/shard_map/ppermute | solution.py:266
  32.7 0.7 %copy-start.4 = (f32[64]{0:T(128)S(1)}, f32[64]{0:T(128)}, u32[]{:S(2)}) copy-start(f32[64]{0:T(128)} %param.11) | copy-start | bytes 772
  32.7 0.7 %copy-start.5 = (f32[64]{0:T(128)S(1)}, f32[64]{0:T(128)}, u32[]{:S(2)}) copy-start(f32[64]{0:T(128)} %param.13) | copy-start | bytes 772
where the time goes:
time: 46.6 us; the launch traced here: 46.2 us
  waiting for transfers between devices  15.3 us (33%)
  Pallas kernels  15.1 us (32%)
  starting transfers between devices  13.7 us (29%)
  other arithmetic  1.24 us (3%)
  local copies, waits for them, and re-layouts  0.7 us (2%)
    pallas_call x1, Pallas kernels, section(): pl.pallas_call(main_kernel, out_shape=jax.ShapeDtypeStruct((32, 2, 32, 12...  12.8 us
    ppermute x1, waiting for transfers between devices, shards(): up_near = lax.ppermute(up_send, 'filt', swap)  9.05 us
    ppermute x1, starting transfers between devices, shards(): far = lax.ppermute(both, 'depth', across)  8.24 us
    ppermute x1, waiting for transfers between devices, shards(): other = lax.ppermute(volume, 'filt', swap)  4.83 us
    ppermute x1, starting transfers between devices, shards(): up_near = lax.ppermute(up_send, 'filt', swap)  2.5 us
    ppermute x1, starting transfers between devices, shards(): other = lax.ppermute(volume, 'filt', swap)  2.12 us
    pallas_call x1, Pallas kernels, prepare_convs(): pl.pallas_call(conv_weight_kernel, out_shape=(jax.ShapeDtypeStruct((384,...  1.47 us
    ppermute x1, waiting for transfers between devices, shards(): near = lax.ppermute(own, 'depth', siblings)  1.44 us
  transfers between devices with their start and end apart: 6, of which 3 were waited for; matrix products, arithmetic and copies ran while one was open for 0% of the time, Pallas kernels for 5%

commit v1 on v0

v1 whole, which is shorter than its diff:
```python
import jax
import jax.numpy as jnp
from jax import lax
from jax.experimental import pallas as pl
from jax.experimental.pallas import tpu as pltpu
from jax.sharding import PartitionSpec as P


F32 = jnp.float32
BF16 = jnp.bfloat16
VMEM = pl.BlockSpec(memory_space=pltpu.VMEM)
SMEM = pl.BlockSpec(memory_space=pltpu.SMEM)
NT = (((1,), (1,)), ((), ()))


def params(mebibytes):
    return pltpu.CompilerParams(vmem_limit_bytes=mebibytes * 2**20)


def cost(flops, count):
    return pl.CostEstimate(flops=flops, bytes_accessed=count, transcendentals=0)


def lanes_of(shape):
    return lax.broadcasted_iota(jnp.int32, shape, len(shape) - 1)


def leaky(value):
    return jnp.where(value > 0, value, 0.2 * value)


def up_weight_kernel(weight_ref, bias_ref, own_ref, send_ref, rows):
    rows[...] = weight_ref[...].astype(F32).T
    for k in range(64):
        block = rows[pl.ds(k, 32, stride=64), :]
        own_ref[k // 32, pl.ds((k % 32) * 32, 32), :] = block.astype(BF16)
    bias = jnp.concatenate([bias_ref[...]] * 4, axis=1)
    high = bias.astype(BF16).astype(F32)
    middle = (bias - high).astype(BF16).astype(F32)
    low = bias - high - middle
    row = lax.broadcasted_iota(jnp.int32, (16, 128), 0)
    parts = jnp.where(row == 0, high, jnp.where(row == 1, middle, jnp.where(row == 2, low, 0.0)))
    for half in range(2):
        own_ref[half, pl.ds(1024, 16), :] = parts.astype(BF16)
    send_ref[...] = own_ref[lax.axis_index("depth") % 2]


def prepare_up(weight, bias_row):
    return pl.pallas_call(
        up_weight_kernel,
        out_shape=(jax.ShapeDtypeStruct((2, 1040, 128), BF16), jax.ShapeDtypeStruct((1040, 128), BF16)),
        in_specs=[VMEM, VMEM],
        out_specs=(VMEM, VMEM),
        scratch_shapes=[pltpu.VMEM((2048, 128), F32)],
        compiler_params=params(12),
        cost_estimate=cost(10**9, 2 * 2**20),
        name="prepare_up",
    )(weight, bias_row)


def conv_weight_kernel(first_ref, second_ref, one_ref, two_ref, spread):
    odd = lax.axis_index("depth") % 2
    lane = lanes_of((1, 128))

    def arrange(source, start, count, out_ref):
        for pair in range(count // 2):
            chunk = source[:, pl.ds(start + pair * 128, 128)].astype(F32)
            spread[pl.ds(2 * pair, 27, stride=64), :] = chunk
            spread[pl.ds(2 * pair + 1, 27, stride=64), :] = pltpu.roll(chunk, 64, 1)
        for eh in range(3):
            for ew in range(3):
                for zp in range(2):
                    for zo in range(2):
                        halves = []
                        for zi in range(2):
                            ed = 2 * zp + zi - zo
                            if 0 <= ed < 3:
                                ed = ed + odd * (2 - 2 * ed)
                                start_row = pl.multiple_of((9 * ed + 3 * eh + ew) * 64, 64)
                                tap = spread[pl.ds(start_row, count), :]
                                halves.append(pltpu.roll(tap, 64, 1) if zi else tap)
                            else:
                                halves.append(jnp.zeros((count, 128), F32))
                        block = jnp.where(lane < 64, halves[0], halves[1])
                        row, column = (ew * 2 + zo) * count, (eh * 2 + zp) * 128
                        out_ref[pl.ds(row, count), pl.ds(column, 128)] = block.astype(BF16)

    arrange(first_ref, 0, 64, one_ref)
    arrange(second_ref, pl.multiple_of(lax.axis_index("filt") * 2048, 2048), 32, two_ref)


def prepare_convs(first, second):
    return pl.pallas_call(
        conv_weight_kernel,
        out_shape=(jax.ShapeDtypeStruct((384, 768), BF16), jax.ShapeDtypeStruct((192, 768), BF16)),
        in_specs=[VMEM, VMEM],
        out_specs=(VMEM, VMEM),
        scratch_shapes=[pltpu.VMEM((27 * 64, 128), F32)],
        compiler_params=params(12),
        cost_estimate=cost(10**9, 2 * 2**20),
        name="prepare_convs",
    )(first, second)


def has_chip_beside():
    depth = lax.axis_index("depth")
    outside = (depth == 0) | (depth == lax.axis_size("depth") - 1)
    return jnp.where(outside, 0.0, 1.0).astype(F32)


def place_plane(plane, ref):
    ref[0:64, :] = jnp.zeros((64, 128), BF16)
    ref[64:1088, :] = plane.T
    ref[1088:1152, :] = jnp.zeros((64, 128), BF16)


def upsample(low_ref, high_ref, weight_ref, bias, zz, a):
    start = a * 64
    lhs = jnp.concatenate(
        [ref[start + hk * 64 : start + hk * 64 + 1024, :] for hk in range(2) for ref in (low_ref, high_ref)], axis=1
    )
    total = lax.dot_general(lhs, weight_ref[a, zz], NT, preferred_element_type=F32)
    width = lax.broadcasted_iota(jnp.int32, (1024, 128), 0) % 64
    aside = total[:, 128:256]
    before = jnp.where(width == 0, 0.0, pltpu.roll(aside, 1, 0))
    after = jnp.where(width == 63, 0.0, pltpu.roll(aside, 1023, 0))
    low_lanes = lanes_of((1024, 128)) < 64
    pair = (before, after) if zz == 0 else (after, before)
    return total[:, 0:128] + jnp.where(low_lanes, *pair) + bias


def interleave(low, high, a, natural):
    low_lanes = lanes_of((1024, 128)) < 64
    even = jnp.where(low_lanes, low, high)
    uneven = pltpu.roll(jnp.where(low_lanes, high, low), 64, 1)
    for h in range(16):
        for b, value in ((0, even), (1, uneven)):
            natural[pl.ds((2 * h + a) * 128 + b, 64, stride=2), :] = value[h * 64 : h * 64 + 64]


def place_pair(natural, ref):
    ref[0:128, :] = jnp.zeros((128, 128), BF16)
    ref[128:4224, :] = natural[...].astype(BF16)
    ref[4224:4352, :] = jnp.zeros((128, 128), BF16)


def column_of(row):
    return jnp.broadcast_to(row, (128, 128)).T


def combine(taps, count, h):
    where = pl.ds(h * 128, 128)
    column = lanes_of((count, 128))
    value = taps[count : 2 * count, where]
    value = value + jnp.where(column == 0, 0.0, pltpu.roll(taps[0:count, where], 1, 1))
    return value + jnp.where(column == 127, 0.0, pltpu.roll(taps[2 * count : 3 * count, where], 127, 1))


def hide(pairs, weight_ref, bias_ref, taps, keep, ref):
    rhs = jnp.concatenate([pair[eh * 128 : eh * 128 + 4096, :] for eh in range(3) for pair in pairs], axis=1)
    taps[...] = lax.dot_general(weight_ref[...], rhs, NT, preferred_element_type=F32)
    row = bias_ref[...]
    bias = column_of(jnp.concatenate([row, row], axis=1))
    ref[:, 0:128] = jnp.zeros((128, 128), BF16)
    ref[:, 4224:4352] = jnp.zeros((128, 128), BF16)
    for h in range(32):
        value = leaky(combine(taps, 128, h) + bias)
        if keep is not None:
            value = value * keep
        ref[:, (h + 1) * 128 : (h + 2) * 128] = value.astype(BF16)


def start_kernel(own_ref, near_ref, up_own_ref, up_near_ref, up_far_ref, up_weight, bias_ref, cells, kept):
    odd = lax.axis_index("depth") % 2
    filt = lax.axis_index("filt")

    for k in range(64):
        kd, kh, kw = 3 - k // 16, 3 - (k // 4) % 4, k % 4
        zin, zz = kd // 2, kd % 2
        hk, a = kh // 2, kh % 2
        place = ((3, 0, 1, 2), (2, 1, 0, 3))[zz][kw]
        half, rest = k // 32, k % 16
        source = pl.ds(pl.multiple_of(((k // 16 % 2 + odd) % 2 * 16 + rest) * 32, 32), 32)
        column = pl.ds((hk * 2 + zin) * 128, 128)
        mine = up_own_ref[(half + odd) % 2, source, :]
        up_weight[a, zz, pl.ds(pl.multiple_of(64 * place + 32 * filt, 32), 32), column] = mine
        theirs = (up_near_ref, up_far_ref)[half][source, :]
        up_weight[a, zz, pl.ds(pl.multiple_of(64 * place + 32 - 32 * filt, 32), 32), column] = theirs

    def bias_of(block):
        parts = block.astype(F32)
        return parts[0:1] + parts[1:2] + parts[2:3]

    mine = bias_of(up_own_ref[0, pl.ds(1024, 16), :])
    theirs = bias_of(up_near_ref[pl.ds(1024, 16), :])
    is_mine = (lanes_of((1, 128)) // 32) % 2 == filt
    bias = jnp.where(is_mine, mine, theirs)
    bias_ref[...] = jnp.broadcast_to(bias, (8, 128))

    place_plane(own_ref[...], cells.at[0])
    place_plane(near_ref[...], cells.at[1])
    for zz in range(2):
        for a in range(2):
            kept[zz, a] = upsample(cells.at[0], cells.at[1], up_weight, bias, zz, a).astype(BF16)


def middle_kernel(far_ref, cells, kept, up_weight, bias_ref, one_ref, bias_one_ref, pair_ref, hidden, near, edge, first, natural, taps):
    keep = has_chip_beside()
    place_plane(far_ref[0], near)
    place_plane(far_ref[1], edge)
    bias = bias_ref[0:1]
    for a in range(2):
        low = upsample(edge, near, up_weight, bias, 0, a) * keep
        high = upsample(near, cells.at[0], up_weight, bias, 1, a) * keep
        interleave(low, high, a, natural)
    place_pair(natural, first)
    for a in range(2):
        low = upsample(near, cells.at[0], up_weight, bias, 0, a)
        interleave(low, kept[1, a].astype(F32), a, natural)
    place_pair(natural, pair_ref)
    upper = lax.broadcasted_iota(jnp.int32, (128, 128), 0) < 64
    hide((first, pair_ref), one_ref, bias_one_ref, taps, jnp.where(upper, keep, 1.0), hidden)


def end_kernel(
    last_ref, cells, kept, up_weight, bias_ref, pair_ref, hidden_ref, one_ref, two_ref, bias_one_ref, bias_two_ref,
    out_ref,
    edge, second, natural, taps, hidden, rows_out,
):
    odd = lax.axis_index("depth") % 2
    place_plane(last_ref[...], edge)
    bias = bias_ref[0:1]
    for a in range(2):
        high = upsample(cells.at[1], edge, up_weight, bias, 1, a)
        interleave(kept[0, a].astype(F32), high, a, natural)
    place_pair(natural, second)
    hide((pair_ref, second), one_ref, bias_one_ref, taps, None, hidden)

    rhs = jnp.concatenate(
        [ref[:, eh * 128 : eh * 128 + 4096] for eh in range(3) for ref in (hidden_ref, hidden)], axis=0
    )
    taps[0:192, :] = jnp.dot(two_ref[...], rhs, preferred_element_type=F32)
    row = bias_two_ref[...]
    row = jnp.where(lax.axis_index("filt") == 0, row[:, 0:32], row[:, 32:64])
    bias = column_of(jnp.concatenate([row] * 4, axis=1))[0:64]
    for h in range(32):
        value = leaky(combine(taps, 64, h) + bias)
        for z in range(2):
            rows_out[pl.ds((z + odd) % 2 * 32 + h, 32, stride=64), :] = value[z * 32 : z * 32 + 32]
    out_ref[...] = rows_out[...].reshape(32, 2, 32, 128).astype(BF16)


def start(*operands):
    return pl.pallas_call(
        start_kernel,
        out_shape=(
            jax.ShapeDtypeStruct((2, 2, 256, 512), BF16),
            jax.ShapeDtypeStruct((8, 128), F32),
            jax.ShapeDtypeStruct((2, 1152, 128), BF16),
            jax.ShapeDtypeStruct((2, 2, 1024, 128), BF16),
        ),
        in_specs=[VMEM] * 5,
        out_specs=(VMEM,) * 4,
        compiler_params=params(16),
        cost_estimate=cost(2 * 10**9, 4 * 2**20),
        name="start",
    )(*operands)


def middle(*operands):
    return pl.pallas_call(
        middle_kernel,
        out_shape=(jax.ShapeDtypeStruct((4352, 128), BF16), jax.ShapeDtypeStruct((128, 4352), BF16)),
        in_specs=[VMEM] * 7,
        out_specs=(VMEM,) * 2,
        scratch_shapes=[
            pltpu.VMEM((1152, 128), BF16),
            pltpu.VMEM((1152, 128), BF16),
            pltpu.VMEM((4352, 128), BF16),
            pltpu.VMEM((4096, 128), F32),
            pltpu.VMEM((384, 4096), F32),
        ],
        compiler_params=params(28),
        cost_estimate=cost(5 * 10**9, 4 * 2**20),
        name="middle",
    )(*operands)


def end(*operands):
    return pl.pallas_call(
        end_kernel,
        out_shape=jax.ShapeDtypeStruct((32, 2, 32, 128), BF16),
        in_specs=[VMEM] * 11,
        out_specs=VMEM,
        scratch_shapes=[
            pltpu.VMEM((1152, 128), BF16),
            pltpu.VMEM((4352, 128), BF16),
            pltpu.VMEM((4096, 128), F32),
            pltpu.VMEM((384, 4096), F32),
            pltpu.VMEM((128, 4352), BF16),
            pltpu.VMEM((2048, 128), F32),
        ],
        compiler_params=params(28),
        cost_estimate=cost(5 * 10**9, 4 * 2**20),
        name="end",
    )(*operands)


def shards(volume, up_weight, up_bias, first_weight, first_bias, second_weight, second_bias):
    devices = lax.axis_size("depth")
    filt = lax.axis_index("filt")
    swap = [(0, 1), (1, 0)]
    siblings = [(i, i ^ 1) for i in range(devices)]
    across = [(i, i + 1) for i in range(1, devices - 1, 2)]
    across = across + [(j, i) for i, j in across]

    other = lax.ppermute(volume, "filt", swap)
    up_own, up_send = prepare_up(up_weight, up_bias[None])
    up_near = lax.ppermute(up_send, "filt", swap)
    up_far = lax.ppermute(up_near, "depth", siblings)
    one, two = prepare_convs(first_weight, second_weight)
    mine = volume.reshape(64, 1024)
    theirs = other.reshape(64, 1024)
    own = jnp.where(filt == 0, jnp.concatenate([mine, theirs]), jnp.concatenate([theirs, mine]))
    near = lax.ppermute(own, "depth", siblings)
    far = lax.ppermute(jnp.stack([own, near]), "depth", across)
    last = lax.ppermute(far[0], "depth", siblings)
    weight, bias, cells, kept = start(own, near, up_own, up_near, up_far)
    pair, hidden = middle(far, cells, kept, weight, bias, one, first_bias[None])
    return end(
        last, cells, kept, weight, bias, pair, hidden, one, two, first_bias[None], second_bias[None]
    )


def solution(mesh):
    placed = (P("filt", "depth", None), P(None, "filt"), P("filt"), P(), P(), P(), P())
    return jax.shard_map(
        shards,
        mesh=mesh,
        in_specs=placed,
        out_specs=P("filt", "depth", None, None),
        check_vma=False,
    )
```

time: 46.6 us -> 45.5 us (0.976); the launches traced: 46.2 us -> 44.7 us
  waiting for transfers between devices: 15.3 us -> 12.1 us
  local copies, waits for them, and re-layouts: 0.7 us -> 1.74 us
  Pallas kernels: 15.1 us -> 15.6 us
    ppermute x1, waiting for transfers between devices: 9.05 us -> 0.01 us  [shards(): up_near = lax.ppermute(up_send, 'filt', swap)]
    ppermute x2, waiting for transfers between devices: 0.01 us -> 7.27 us  [the longest x1 7.26 us: shards(): far = lax.ppermute(jnp.stack([own, near]), 'depth', across)]
    ppermute x1, waiting for transfers between devices: 1.44 us -> 0.01 us  [shards(): near = lax.ppermute(own, 'depth', siblings)]
    unnamed x14, local copies, waits for them, and re-layouts: 0.68 us -> 1.72 us
    pallas_call x1 -> x3, Pallas kernels: 12.8 us -> 13.2 us  [the longest x1 6.48 us: end(): pl.pallas_call(end_kernel, out_shape=jax.ShapeDtypeStruct((32, 2, 32, 128...]
  transfers between devices with their start and end apart: 6 -> 6, of which waited for: 3 -> 2; matrix products, arithmetic and copies ran while one was open for 0% -> 0% of each run, Pallas kernels for 5% -> 20%
where the time goes in v1:
time: 45.5 us; the launch traced here: 44.7 us
  Pallas kernels  15.6 us (34%)
  starting transfers between devices  13.9 us (31%)
  waiting for transfers between devices  12.1 us (27%)
  local copies, waits for them, and re-layouts  1.74 us (4%)
  other arithmetic  1.14 us (3%)
    ppermute x1, starting transfers between devices, shards(): far = lax.ppermute(jnp.stack([own, near]), 'depth', across)  9.09 us
    ppermute x1, waiting for transfers between devices, shards(): far = lax.ppermute(jnp.stack([own, near]), 'depth', across)  7.26 us
    pallas_call x1, Pallas kernels, end(): pl.pallas_call(end_kernel, out_shape=jax.ShapeDtypeStruct((32, 2, 32, 128...  6.48 us
    pallas_call x1, Pallas kernels, middle(): pl.pallas_call(middle_kernel, out_shape=(jax.ShapeDtypeStruct((4352, 128)...  5.23 us
    ppermute x1, waiting for transfers between devices, shards(): other = lax.ppermute(volume, 'filt', swap)  4.83 us
    ppermute x1, starting transfers between devices, shards(): up_near = lax.ppermute(up_send, 'filt', swap)  2.2 us
    ppermute x1, starting transfers between devices, shards(): other = lax.ppermute(volume, 'filt', swap)  2.12 us
    unnamed x14, local copies, waits for them, and re-layouts  1.72 us
  transfers between devices with their start and end apart: 6, of which 2 were waited for; matrix products, arithmetic and copies ran while one was open for 0% of the time, Pallas kernels for 20%

profile of v1, /device:TPU:2, one launch (start us, length us, event | category | flops | bytes accessed | tf_op | source)
XLA Modules:
  0.0 44.7 jit_solution(1761497068453395221)
XLA Ops:
  0.0 2.1 %collective-permute-start = (bf16[64,1,1024]{2,0,1:T(8,128)(2,1)}, bf16[64,1,1024]{2,0,1:T(8,128)(2,1)S(1)}, u32[]{:S(2)}, u32[]{:S(2)}) collective-permute-start(bf16[64,1,1024]{2,0,1:T(8,128)(2,1)} %param.7), channel_id=1, source_target_pairs={{0,1},{1,0},{2,3},{3,2},{4,5},{5,4},{6,7},{7,6},{8,9},{9,8},{10,11... | collective-permute-start | bytes 393224 | tf_op jit(solution)/shard_map/ppermute | solution.py:317
  2.1 4.8 %collective-permute-done = bf16[64,1,1024]{2,0,1:T(8,128)(2,1)S(1)} collective-permute-done((bf16[64,1,1024]{2,0,1:T(8,128)(2,1)}, bf16[64,1,1024]{2,0,1:T(8,128)(2,1)S(1)}, u32[]{:S(2)}, u32[]{:S(2)}) %collective-permute-start) | collective-permute-done | bytes 131104 | tf_op jit(solution)/shard_map/ppermute | solution.py:317
  7.0 1.0 %maximum_select_fusion.1.own_ref = bf16[128,1024]{1,0:T(8,128)(2,1)S(1)} fusion(bf16[64,1024]{1,0:T(8,128)(2,1)S(1)} %bitcast.17, bf16[64,1024]{1,0:T(8,128)(2,1)} %bitcast.15, pred[]{:T(512)S(6)} %eq.3), kind=kLoop, calls=%fused_computation.3 | loop fusion | flops 1179648 | bytes 524289 | tf_op jit(solution)/shard_map/jit(_where)/select_n | solution.py:324
  8.0 0.1 collective-permute-start.1
  8.1 0.0 copy-start
  8.1 1.0 %copy-done = bf16[128,2048]{1,0:T(8,128)(2,1)S(1)} copy-done((bf16[128,2048]{1,0:T(8,128)(2,1)S(1)}, bf16[128,2048]{1,0:T(8,128)(2,1)}, u32[]{:S(2)}) %copy-start) | copy-done | bytes 524312
  9.1 0.0 copy-start.3
  9.1 0.7 %copy-done.3 = f32[32]{0:T(128)S(1)} copy-done((f32[32]{0:T(128)S(1)}, f32[32]{0:T(128)}, u32[]{:S(2)}) %copy-start.3) | copy-done | bytes 152
  9.8 0.8 %prepare_up.1 = (bf16[2,1040,128]{2,1,0:T(8,128)(2,1)S(1)}, bf16[1040,128]{1,0:T(8,128)(2,1)S(1)}) custom-call(bf16[128,2048]{1,0:T(8,128)(2,1)S(1)} %copy-done, f32[1,32]{1,0:T(1,128)S(1)} %bitcast.11), custom_call_target="tpu_custom_call" | custom-call | flops 1000000000 | bytes 2097152 | tf_op jit(solution)/shard_map/prepare_up/pallas_call | solution.py:49
  10.6 0.0 copy-start.1
  10.6 0.0 copy-start.2
  10.6 2.2 %collective-permute-start.4 = (bf16[1040,128]{1,0:T(8,128)(2,1)S(1)}, bf16[1040,128]{1,0:T(8,128)(2,1)S(1)}, u32[]{:S(2)}, u32[]{:S(2)}) collective-permute-start(bf16[1040,128]{1,0:T(8,128)(2,1)S(1)} %get-tuple-element.16), channel_id=1, source_target_pairs={{0,1},{1,0},{2,3},{3,2},{4,5},{5,4},{6,7},{7,6},{8,9},{9,8},{10,11... | collective-permute-start | bytes 798728 | tf_op jit(solution)/shard_map/ppermute | solution.py:319
  12.9 0.0 copy-done.6
  12.9 0.0 collective-permute-done.1.near_ref
  12.9 0.1 pad_maximum_fusion
  13.0 9.1 %collective-permute-start.2 = (bf16[2,128,1024]{2,1,0:T(8,128)(2,1)S(1)}, bf16[2,128,1024]{2,1,0:T(8,128)(2,1)S(1)}, u32[]{:S(2)}, u32[]{:S(2)}) collective-permute-start(bf16[2,128,1024]{2,1,0:T(8,128)(2,1)S(1)} %pad_maximum_fusion), channel_id=1, source_target_pairs={{2,4},{6,8},{10,12},{14,16},{18,20},{22,24},{26,28},{30,32},{34,36... | collective-permute-start | bytes 1572872 | tf_op jit(solution)/shard_map/ppermute | solution.py:326
  22.1 0.0 collective-permute-done.4.up_near_ref
  22.1 0.1 collective-permute-start.5
  22.2 0.0 copy-done.1
  22.2 0.0 copy-done.2
  22.2 1.6 %prepare_convs.1 = (bf16[384,768]{1,0:T(8,128)(2,1)S(1)}, bf16[192,768]{1,0:T(8,128)(2,1)S(1)}) custom-call(bf16[27,4096]{1,0:T(8,128)(2,1)S(1)} %copy-done.1, bf16[27,4096]{1,0:T(8,128)(2,1)S(1)} %copy-done.2), custom_call_target="tpu_custom_call" | custom-call | flops 1000000000 | bytes 2097152 | tf_op jit(solution)/shard_map/prepare_convs/pallas_call | solution.py:93
  23.8 0.0 collective-permute-done.5.up_far_ref
  23.8 0.0 copy-start.4
  23.8 1.5 %start.1 = (bf16[2,2,256,512]{3,2,1,0:T(8,128)(2,1)S(1)}, f32[8,128]{1,0:T(8,128)S(1)}, bf16[2,1152,128]{2,1,0:T(8,128)(2,1)S(1)}, bf16[2,2,1024,128]{3,2,1,0:T(8,128)(2,1)S(1)}) custom-call(bf16[128,1024]{1,0:T(8,128)(2,1)S(1)} %maximum_select_fusion.1.own_ref, bf16[128,1024]{1,0:T(8,128)(2,1)S(1)} %collective-permute-done.1.near_ref, ...), custom_call_target="tpu_custom_call" | custom-call | flops 2000000000 | bytes 4194304 | tf_op jit(solution)/shard_map/start/pallas_call | solution.py:254
  25.3 7.3 %collective-permute-done.2.far_ref = bf16[2,128,1024]{2,1,0:T(8,128)(2,1)S(1)} collective-permute-done((bf16[2,128,1024]{2,1,0:T(8,128)(2,1)S(1)}, bf16[2,128,1024]{2,1,0:T(8,128)(2,1)S(1)}, u32[]{:S(2)}, u32[]{:S(2)}) %collective-permute-start.2) | collective-permute-done | bytes 524320 | tf_op jit(solution)/shard_map/ppermute | solution.py:326
  32.6 0.3 collective-permute-start.3
  32.9 0.0 copy-done.4
  32.9 0.0 copy-start.5
  32.9 5.2 %middle.1 = (bf16[4352,128]{1,0:T(8,128)(2,1)S(1)}, bf16[128,4352]{1,0:T(8,128)(2,1)S(1)}) custom-call(bf16[2,128,1024]{2,1,0:T(8,128)(2,1)S(1)} %collective-permute-done.2.far_ref, bf16[2,1152,128]{2,1,0:T(8,128)(2,1)S(1)} %get-tuple-element.17.cells, bf16[2,2,1024,128]{3,2,1,0:T(8,128)(2,1)S(1)} %get-tuple-element.18.kept, ...), custom_call_target="tpu_custom_call" | custom-call | flops 5000000000 | bytes 4194304 | tf_op jit(solution)/shard_map/middle/pallas_call | solution.py:271
  38.2 0.0 collective-permute-done.3.last_ref
  38.2 0.0 copy-done.5
  38.2 6.5 %end.1 = bf16[32,2,32,128]{3,2,1,0:T(8,128)(2,1)} custom-call(bf16[128,1024]{1,0:T(8,128)(2,1)S(1)} %collective-permute-done.3.last_ref, bf16[2,1152,128]{2,1,0:T(8,128)(2,1)S(1)} %get-tuple-element.17.cells, bf16[2,2,1024,128]{3,2,1,0:T(8,128)(2,1)S(1)} %get-tuple-element.18.kept, bf16[2,2,256,512]{3,2,1,0:T(8,128)(2,1)S(1)} %get-tuple-element.19.up_weight, ...), custom_call_target="tpu_custom_call" | custom-call | flops 5000000000 | bytes 4194304 | tf_op jit(solution)/shard_map/end/pallas_call | solution.py:290
  (3 shorter events, 0.1 us)
Async XLA Ops:
  0.0 7.0 %collective-permute-start = (bf16[64,1,1024]{2,0,1:T(8,128)(2,1)}, bf16[64,1,1024]{2,0,1:T(8,128)(2,1)S(1)}, u32[]{:S(2)}, u32[]{:S(2)}) collective-permute-start(bf16[64,1,1024]{2,0,1:T(8,128)(2,1)} %param.7), channel_id=1, source_target_pairs={{0,1},{1,0},{2,3},{3,2},{4,5},{5,4},{6,7},{7,6},{8,9},{9,8},{10,11... | collective-permute-start | bytes 393224 | tf_op jit(solution)/shard_map/ppermute | solution.py:317
  8.0 4.9 %collective-permute-start.1 = (bf16[128,1024]{1,0:T(8,128)(2,1)S(1)}, bf16[128,1024]{1,0:T(8,128)(2,1)S(1)}, u32[]{:S(2)}, u32[]{:S(2)}) collective-permute-start(bf16[128,1024]{1,0:T(8,128)(2,1)S(1)} %maximum_select_fusion.1.own_ref), channel_id=1, source_target_pairs={{0,2},{2,0},{4,6},{6,4},{8,10},{10,8},{12,14},{14,12},{16,18},{18,... | collective-permute-start | bytes 786440 | tf_op jit(solution)/shard_map/ppermute | solution.py:325
  8.1 1.0 %copy-start = (bf16[128,2048]{1,0:T(8,128)(2,1)S(1)}, bf16[128,2048]{1,0:T(8,128)(2,1)}, u32[]{:S(2)}) copy-start(bf16[128,2048]{1,0:T(8,128)(2,1)} %weight_ref.1) | copy-start | bytes 1572868
  9.1 0.7 %copy-start.3 = (f32[32]{0:T(128)S(1)}, f32[32]{0:T(128)}, u32[]{:S(2)}) copy-start(f32[32]{0:T(128)} %param.9) | copy-start | bytes 388
  9.8 3.1 %copy-start.6 = (bf16[64,1,1024]{2,0,1:T(8,128)(2,1)S(1)}, bf16[64,1,1024]{2,0,1:T(8,128)(2,1)}, u32[]{:S(2)}) copy-start(bf16[64,1,1024]{2,0,1:T(8,128)(2,1)} %param.7) | copy-start | bytes 393220
  10.6 11.6 %copy-start.1 = (bf16[27,4096]{1,0:T(8,128)(2,1)S(1)}, bf16[27,4096]{1,0:T(8,128)(2,1)}, u32[]{:S(2)}) copy-start(bf16[27,4096]{1,0:T(8,128)(2,1)} %first_ref.1) | copy-start | bytes 663556
  10.6 11.6 %copy-start.2 = (bf16[27,4096]{1,0:T(8,128)(2,1)S(1)}, bf16[27,4096]{1,0:T(8,128)(2,1)}, u32[]{:S(2)}) copy-start(bf16[27,4096]{1,0:T(8,128)(2,1)} %second_ref.1) | copy-start | bytes 663556
  10.6 11.4 %collective-permute-start.4 = (bf16[1040,128]{1,0:T(8,128)(2,1)S(1)}, bf16[1040,128]{1,0:T(8,128)(2,1)S(1)}, u32[]{:S(2)}, u32[]{:S(2)}) collective-permute-start(bf16[1040,128]{1,0:T(8,128)(2,1)S(1)} %get-tuple-element.16), channel_id=1, source_target_pairs={{0,1},{1,0},{2,3},{3,2},{4,5},{5,4},{6,7},{7,6},{8,9},{9,8},{10,11... | collective-permute-start | bytes 798728 | tf_op jit(solution)/shard_map/ppermute | solution.py:319
  13.0 19.6 %collective-permute-start.2 = (bf16[2,128,1024]{2,1,0:T(8,128)(2,1)S(1)}, bf16[2,128,1024]{2,1,0:T(8,128)(2,1)S(1)}, u32[]{:S(2)}, u32[]{:S(2)}) collective-permute-start(bf16[2,128,1024]{2,1,0:T(8,128)(2,1)S(1)} %pad_maximum_fusion), channel_id=1, source_target_pairs={{2,4},{6,8},{10,12},{14,16},{18,20},{22,24},{26,28},{30,32},{34,36... | collective-permute-start | bytes 1572872 | tf_op jit(solution)/shard_map/ppermute | solution.py:326
  22.1 1.7 %collective-permute-start.5 = (bf16[1040,128]{1,0:T(8,128)(2,1)S(1)}, bf16[1040,128]{1,0:T(8,128)(2,1)S(1)}, u32[]{:S(2)}, u32[]{:S(2)}) collective-permute-start(bf16[1040,128]{1,0:T(8,128)(2,1)S(1)} %collective-permute-done.4.up_near_ref), channel_id=1, source_target_pairs={{0,2},{2,0},{4,6},{6,4},{8,10},{10,8},{12,14},{14,12},{16,18},{18,... | collective-permute-start | bytes 798728 | tf_op jit(solution)/shard_map/ppermute | solution.py:320
  23.8 9.1 %copy-start.4 = (f32[64]{0:T(128)S(1)}, f32[64]{0:T(128)}, u32[]{:S(2)}) copy-start(f32[64]{0:T(128)} %param.11) | copy-start | bytes 772
  32.6 5.5 %collective-permute-start.3 = (bf16[128,1024]{1,0:T(8,128)(2,1)S(1)}, bf16[128,1024]{1,0:T(8,128)(2,1)S(1)}, u32[]{:S(2)}, u32[]{:S(2)}) collective-permute-start(bf16[128,1024]{1,0:T(8,128)(2,1)S(1)} %slice_bitcast_fusion), channel_id=1, source_target_pairs={{0,2},{2,0},{4,6},{6,4},{8,10},{10,8},{12,14},{14,12},{16,18},{18,... | collective-permute-start | bytes 786440 | tf_op jit(solution)/shard_map/ppermute | solution.py:327
  32.9 5.3 %copy-start.5 = (f32[64]{0:T(128)S(1)}, f32[64]{0:T(128)}, u32[]{:S(2)}) copy-start(f32[64]{0:T(128)} %param.13) | copy-start | bytes 772

commit v2 on v1

--- a/solution.py
+++ b/solution.py
@@ -204,30 +204,21 @@
             kept[zz, a] = upsample(cells.at[0], cells.at[1], up_weight, bias, zz, a).astype(BF16)
 
 
-def middle_kernel(far_ref, cells, kept, up_weight, bias_ref, one_ref, bias_one_ref, pair_ref, hidden, near, edge, first, natural, taps):
-    keep = has_chip_beside()
-    place_plane(far_ref[0], near)
-    place_plane(far_ref[1], edge)
+def middle_kernel(next_ref, cells, kept, up_weight, bias_ref, near, pair_ref, low_kept, natural):
+    place_plane(next_ref[...], near)
     bias = bias_ref[0:1]
     for a in range(2):
-        low = upsample(edge, near, up_weight, bias, 0, a) * keep
-        high = upsample(near, cells.at[0], up_weight, bias, 1, a) * keep
-        interleave(low, high, a, natural)
-    place_pair(natural, first)
-    for a in range(2):
+        low_kept[a] = upsample(near, cells.at[0], up_weight, bias, 1, a).astype(BF16)
         low = upsample(near, cells.at[0], up_weight, bias, 0, a)
         interleave(low, kept[1, a].astype(F32), a, natural)
     place_pair(natural, pair_ref)
-    upper = lax.broadcasted_iota(jnp.int32, (128, 128), 0) < 64
-    hide((first, pair_ref), one_ref, bias_one_ref, taps, jnp.where(upper, keep, 1.0), hidden)
-
-
-def end_kernel(
-    last_ref, cells, kept, up_weight, bias_ref, pair_ref, hidden_ref, one_ref, two_ref, bias_one_ref, bias_two_ref,
-    out_ref,
-    edge, second, natural, taps, hidden, rows_out,
+
+
+def late_kernel(
+    last_ref, cells, kept, up_weight, bias_ref, pair_ref, one_ref, bias_one_ref,
+    hidden,
+    edge, second, natural, taps,
 ):
-    odd = lax.axis_index("depth") % 2
     place_plane(last_ref[...], edge)
     bias = bias_ref[0:1]
     for a in range(2):
@@ -236,8 +227,25 @@
     place_pair(natural, second)
     hide((pair_ref, second), one_ref, bias_one_ref, taps, None, hidden)
 
+
+def end_kernel(
+    after_ref, near, low_kept, up_weight, bias_ref, pair_ref, hidden_ref, one_ref, two_ref, bias_one_ref, bias_two_ref,
+    out_ref,
+    edge, first, natural, taps, hidden, rows_out,
+):
+    odd = lax.axis_index("depth") % 2
+    keep = has_chip_beside()
+    place_plane(after_ref[...], edge)
+    bias = bias_ref[0:1]
+    for a in range(2):
+        low = upsample(edge, near, up_weight, bias, 0, a) * keep
+        interleave(low, low_kept[a].astype(F32) * keep, a, natural)
+    place_pair(natural, first)
+    upper = lax.broadcasted_iota(jnp.int32, (128, 128), 0) < 64
+    hide((first, pair_ref), one_ref, bias_one_ref, taps, jnp.where(upper, keep, 1.0), hidden)
+
     rhs = jnp.concatenate(
-        [ref[:, eh * 128 : eh * 128 + 4096] for eh in range(3) for ref in (hidden_ref, hidden)], axis=0
+        [ref[:, eh * 128 : eh * 128 + 4096] for eh in range(3) for ref in (hidden, hidden_ref)], axis=0
     )
     taps[0:192, :] = jnp.dot(two_ref[...], rhs, preferred_element_type=F32)
     row = bias_two_ref[...]
@@ -270,11 +278,27 @@
 def middle(*operands):
     return pl.pallas_call(
         middle_kernel,
-        out_shape=(jax.ShapeDtypeStruct((4352, 128), BF16), jax.ShapeDtypeStruct((128, 4352), BF16)),
-        in_specs=[VMEM] * 7,
-        out_specs=(VMEM,) * 2,
+        out_shape=(
+            jax.ShapeDtypeStruct((1152, 128), BF16),
+            jax.ShapeDtypeStruct((4352, 128), BF16),
+            jax.ShapeDtypeStruct((2, 1024, 128), BF16),
+        ),
+        in_specs=[VMEM] * 5,
+        out_specs=(VMEM,) * 3,
+        scratch_shapes=[pltpu.VMEM((4096, 128), F32)],
+        compiler_params=params(16),
+        cost_estimate=cost(2 * 10**9, 4 * 2**20),
+        name="middle",
+    )(*operands)
+
+
+def late(*operands):
+    return pl.pallas_call(
+        late_kernel,
+        out_shape=jax.ShapeDtypeStruct((128, 4352), BF16),
+        in_specs=[VMEM] * 8,
+        out_specs=VMEM,
         scratch_shapes=[
-            pltpu.VMEM((1152, 128), BF16),
             pltpu.VMEM((1152, 128), BF16),
             pltpu.VMEM((4352, 128), BF16),
             pltpu.VMEM((4096, 128), F32),
@@ -282,7 +306,7 @@
         ],
         compiler_params=params(28),
         cost_estimate=cost(5 * 10**9, 4 * 2**20),
-        name="middle",
+        name="late",
     )(*operands)
 
 
@@ -314,22 +338,21 @@
     across = [(i, i + 1) for i in range(1, devices - 1, 2)]
     across = across + [(j, i) for i, j in across]
 
-    other = lax.ppermute(volume, "filt", swap)
+    mine = volume.reshape(64, 1024)
+    theirs = lax.ppermute(mine, "filt", swap)
     up_own, up_send = prepare_up(up_weight, up_bias[None])
     up_near = lax.ppermute(up_send, "filt", swap)
+    own = jnp.where(filt == 0, jnp.concatenate([mine, theirs]), jnp.concatenate([theirs, mine]))
+    beyond = lax.ppermute(own, "depth", across)
+    near = lax.ppermute(own, "depth", siblings)
+    after = lax.ppermute(near, "depth", across)
     up_far = lax.ppermute(up_near, "depth", siblings)
+    last = lax.ppermute(beyond, "depth", siblings)
     one, two = prepare_convs(first_weight, second_weight)
-    mine = volume.reshape(64, 1024)
-    theirs = other.reshape(64, 1024)
-    own = jnp.where(filt == 0, jnp.concatenate([mine, theirs]), jnp.concatenate([theirs, mine]))
-    near = lax.ppermute(own, "depth", siblings)
-    far = lax.ppermute(jnp.stack([own, near]), "depth", across)
-    last = lax.ppermute(far[0], "depth", siblings)
     weight, bias, cells, kept = start(own, near, up_own, up_near, up_far)
-    pair, hidden = middle(far, cells, kept, weight, bias, one, first_bias[None])
-    return end(
-        last, cells, kept, weight, bias, pair, hidden, one, two, first_bias[None], second_bias[None]
-    )
+    next_cells, pair, low_kept = middle(beyond, cells, kept, weight, bias)
+    hidden = late(last, cells, kept, weight, bias, pair, one, first_bias[None])
+    return end(after, next_cells, low_kept, weight, bias, pair, hidden, one, two, first_bias[None], second_bias[None])
 
 
 def solution(mesh):

time: 45.5 us -> 48.1 us (1.057)
  starting transfers between devices: 13.9 us -> 17.8 us
  other arithmetic: 1.14 us -> 0.05 us
    ppermute x1, waiting for transfers between devices: 0.01 us -> 7.24 us  [shards(): up_near = lax.ppermute(up_send, 'filt', swap)]
    ppermute x3 -> x4, waiting for transfers between devices: 12.1 us -> 4.91 us  [the longest x1 3.23 us: shards(): beyond = lax.ppermute(own, 'depth', across)]
    ppermute x3 -> x4, starting transfers between devices: 11.5 us -> 15.5 us  [the longest x1 7.13 us: shards(): after = lax.ppermute(near, 'depth', across)]
    select_n x2 -> x1, other arithmetic: 1.09 us -> 0.05 us  [shards(): jnp.where(filt == 0, jnp.concatenate([mine, theirs]), jnp.concatenate([th...]
    pallas_call x1 -> x2, Pallas kernels: 5.23 us -> 5.43 us  [the longest x1 3.87 us: late(): pl.pallas_call(late_kernel, out_shape=jax.ShapeDtypeStruct((128, 4352), B...]
  transfers between devices with their start and end apart: 6 -> 7, of which waited for: 2 -> 3; matrix products, arithmetic and copies ran while one was open for 0% -> 0% of each run, Pallas kernels for 20% -> 18%
where the time goes in v2:
time: 48.1 us; the launch traced here: 47.6 us
  starting transfers between devices  17.8 us (37%)
  Pallas kernels  15.7 us (33%)
  waiting for transfers between devices  12.2 us (25%)
  local copies, waits for them, and re-layouts  1.72 us (4%)
    ppermute x1, waiting for transfers between devices, shards(): up_near = lax.ppermute(up_send, 'filt', swap)  7.24 us
    ppermute x1, starting transfers between devices, shards(): after = lax.ppermute(near, 'depth', across)  7.13 us
    ppermute x1, starting transfers between devices, shards(): beyond = lax.ppermute(own, 'depth', across)  6.96 us
    pallas_call x1, Pallas kernels, end(): pl.pallas_call(end_kernel, out_shape=jax.ShapeDtypeStruct((32, 2, 32, 128...  6.39 us
    pallas_call x1, Pallas kernels, late(): pl.pallas_call(late_kernel, out_shape=jax.ShapeDtypeStruct((128, 4352), B...  3.87 us
    ppermute x1, waiting for transfers between devices, shards(): beyond = lax.ppermute(own, 'depth', across)  3.23 us
    ppermute x1, starting transfers between devices, shards(): up_near = lax.ppermute(up_send, 'filt', swap)  2.2 us
    unnamed x14, local copies, waits for them, and re-layouts  1.72 us
  transfers between devices with their start and end apart: 7, of which 3 were waited for; matrix products, arithmetic and copies ran while one was open for 0% of the time, Pallas kernels for 18%

profile of v2, /device:TPU:2, one launch (start us, length us, event | category | flops | bytes accessed | tf_op | source)
XLA Modules:
  0.0 47.6 jit_solution(13396179803669390287)
XLA Ops:
  0.0 0.0 copy-start
  0.0 1.0 %copy-done = bf16[128,2048]{1,0:T(8,128)(2,1)S(1)} copy-done((bf16[128,2048]{1,0:T(8,128)(2,1)S(1)}, bf16[128,2048]{1,0:T(8,128)(2,1)}, u32[]{:S(2)}) %copy-start) | copy-done | bytes 524312
  1.0 0.0 copy-start.3
  1.0 0.7 %copy-done.3 = f32[32]{0:T(128)S(1)} copy-done((f32[32]{0:T(128)S(1)}, f32[32]{0:T(128)}, u32[]{:S(2)}) %copy-start.3) | copy-done | bytes 152
  1.7 0.0 copy-start.6
  1.7 0.8 %prepare_up.1 = (bf16[2,1040,128]{2,1,0:T(8,128)(2,1)S(1)}, bf16[1040,128]{1,0:T(8,128)(2,1)S(1)}) custom-call(bf16[128,2048]{1,0:T(8,128)(2,1)S(1)} %copy-done, f32[1,32]{1,0:T(1,128)S(1)} %bitcast.4), custom_call_target="tpu_custom_call" | custom-call | flops 1000000000 | bytes 2097152 | tf_op jit(solution)/shard_map/prepare_up/pallas_call | solution.py:49
  2.5 2.2 %collective-permute-start.4 = (bf16[1040,128]{1,0:T(8,128)(2,1)S(1)}, bf16[1040,128]{1,0:T(8,128)(2,1)S(1)}, u32[]{:S(2)}, u32[]{:S(2)}) collective-permute-start(bf16[1040,128]{1,0:T(8,128)(2,1)S(1)} %get-tuple-element.17), channel_id=1, source_target_pairs={{0,1},{1,0},{2,3},{3,2},{4,5},{5,4},{6,7},{7,6},{8,9},{9,8},{10,11... | collective-permute-start | bytes 798728 | tf_op jit(solution)/shard_map/ppermute | solution.py:344
  4.7 0.0 copy-done.6
  4.7 1.4 %collective-permute-start = (bf16[64,1024]{1,0:T(8,128)(2,1)S(1)}, bf16[64,1024]{1,0:T(8,128)(2,1)S(1)}, u32[]{:S(2)}, u32[]{:S(2)}) collective-permute-start(bf16[64,1024]{1,0:T(8,128)(2,1)S(1)} %bitcast.8), channel_id=1, source_target_pairs={{0,1},{1,0},{2,3},{3,2},{4,5},{5,4},{6,7},{7,6},{8,9},{9,8},{10,11... | collective-permute-start | bytes 393224 | tf_op jit(solution)/shard_map/ppermute | solution.py:342
  6.1 7.2 %collective-permute-done.4.up_near_ref = bf16[1040,128]{1,0:T(8,128)(2,1)S(1)} collective-permute-done((bf16[1040,128]{1,0:T(8,128)(2,1)S(1)}, bf16[1040,128]{1,0:T(8,128)(2,1)S(1)}, u32[]{:S(2)}, u32[]{:S(2)}) %collective-permute-start.4) | collective-permute-done | bytes 266272 | tf_op jit(solution)/shard_map/ppermute | solution.py:344
  13.4 0.0 collective-permute-start.5
  13.4 1.7 %collective-permute-done = bf16[64,1024]{1,0:T(8,128)(2,1)S(1)} collective-permute-done((bf16[64,1024]{1,0:T(8,128)(2,1)S(1)}, bf16[64,1024]{1,0:T(8,128)(2,1)S(1)}, u32[]{:S(2)}, u32[]{:S(2)}) %collective-permute-start) | collective-permute-done | bytes 131104 | tf_op jit(solution)/shard_map/ppermute | solution.py:342
  15.1 7.0 %collective-permute-start.3 = (bf16[128,1024]{1,0:T(8,128)(2,1)S(1)}, bf16[128,1024]{1,0:T(8,128)(2,1)S(1)}, u32[]{:S(2)}, u32[]{:S(2)}) collective-permute-start(bf16[128,1024]{1,0:T(8,128)(2,1)S(1)} %maximum_select_fusion.own_ref), channel_id=1, source_target_pairs={{2,4},{6,8},{10,12},{14,16},{18,20},{22,24},{26,28},{30,32},{34,36... | collective-permute-start | bytes 786440 | tf_op jit(solution)/shard_map/ppermute | solution.py:346
  22.1 0.1 collective-permute-start.1
  22.2 0.0 copy-done.1
  22.2 0.0 copy-done.2
  22.2 1.6 %prepare_convs.1 = (bf16[384,768]{1,0:T(8,128)(2,1)S(1)}, bf16[192,768]{1,0:T(8,128)(2,1)S(1)}) custom-call(bf16[27,4096]{1,0:T(8,128)(2,1)S(1)} %copy-done.1, bf16[27,4096]{1,0:T(8,128)(2,1)S(1)} %copy-done.2), custom_call_target="tpu_custom_call" | custom-call | flops 1000000000 | bytes 2097152 | tf_op jit(solution)/shard_map/prepare_convs/pallas_call | solution.py:93
  23.8 3.2 %collective-permute-done.3.next_ref = bf16[128,1024]{1,0:T(8,128)(2,1)S(1)} collective-permute-done((bf16[128,1024]{1,0:T(8,128)(2,1)S(1)}, bf16[128,1024]{1,0:T(8,128)(2,1)S(1)}, u32[]{:S(2)}, u32[]{:S(2)}) %collective-permute-start.3) | collective-permute-done | bytes 262176 | tf_op jit(solution)/shard_map/ppermute | solution.py:346
  27.0 0.0 collective-permute-start.6
  27.0 0.0 collective-permute-done.1.near_ref
  27.0 7.1 %collective-permute-start.2 = (bf16[128,1024]{1,0:T(8,128)(2,1)S(1)}, bf16[128,1024]{1,0:T(8,128)(2,1)S(1)}, u32[]{:S(2)}, u32[]{:S(2)}) collective-permute-start(bf16[128,1024]{1,0:T(8,128)(2,1)S(1)} %collective-permute-done.1.near_ref), channel_id=1, source_target_pairs={{2,4},{6,8},{10,12},{14,16},{18,20},{22,24},{26,28},{30,32},{34,36... | collective-permute-start | bytes 786440 | tf_op jit(solution)/shard_map/ppermute | solution.py:348
  34.2 0.0 collective-permute-done.5.up_far_ref
  34.2 1.5 %start.1 = (bf16[2,2,256,512]{3,2,1,0:T(8,128)(2,1)S(1)}, f32[8,128]{1,0:T(8,128)S(1)}, bf16[2,1152,128]{2,1,0:T(8,128)(2,1)S(1)}, bf16[2,2,1024,128]{3,2,1,0:T(8,128)(2,1)S(1)}) custom-call(bf16[128,1024]{1,0:T(8,128)(2,1)S(1)} %maximum_select_fusion.own_ref, bf16[128,1024]{1,0:T(8,128)(2,1)S(1)} %collective-permute-done.1.near_ref, ...), custom_call_target="tpu_custom_call" | custom-call | flops 2000000000 | bytes 4194304 | tf_op jit(solution)/shard_map/start/pallas_call | solution.py:262
  35.7 0.0 copy-start.4
  35.7 1.6 %middle.1 = (bf16[1152,128]{1,0:T(8,128)(2,1)S(1)}, bf16[4352,128]{1,0:T(8,128)(2,1)S(1)}, bf16[2,1024,128]{2,1,0:T(8,128)(2,1)S(1)}) custom-call(bf16[128,1024]{1,0:T(8,128)(2,1)S(1)} %collective-permute-done.3.next_ref, bf16[2,1152,128]{2,1,0:T(8,128)(2,1)S(1)} %get-tuple-element.18.cells, bf16[2,2,1024,128]{3,2,1,0:T(8,128)(2,1)S(1)} %get-tuple-element.19.kept, ...), custom_call_target="tpu_custom_call" | custom-call | flops 2000000000 | bytes 4194304 | tf_op jit(solution)/shard_map/middle/pallas_call | solution.py:279
  37.3 0.0 collective-permute-done.6.last_ref
  37.3 0.0 copy-done.4
  37.3 0.0 copy-start.5
  37.3 3.9 %late.1.hidden_ref = bf16[128,4352]{1,0:T(8,128)(2,1)S(1)} custom-call(bf16[128,1024]{1,0:T(8,128)(2,1)S(1)} %collective-permute-done.6.last_ref, bf16[2,1152,128]{2,1,0:T(8,128)(2,1)S(1)} %get-tuple-element.18.cells, bf16[2,2,1024,128]{3,2,1,0:T(8,128)(2,1)S(1)} %get-tuple-element.19.kept, bf16[2,2,256,512]{3,2,1,0:T(8,128)(2,1)S(1)} %get-tuple-element.20.up_weight, ...), custom_call_target="tpu_custom_call" | custom-call | flops 5000000000 | bytes 4194304 | tf_op jit(solution)/shard_map/late/pallas_call | solution.py:296
  41.2 0.0 collective-permute-done.2.after_ref
  41.2 0.0 copy-done.5
  41.2 6.4 %end.1 = bf16[32,2,32,128]{3,2,1,0:T(8,128)(2,1)} custom-call(bf16[128,1024]{1,0:T(8,128)(2,1)S(1)} %collective-permute-done.2.after_ref, bf16[1152,128]{1,0:T(8,128)(2,1)S(1)} %get-tuple-element.22.near, bf16[2,1024,128]{2,1,0:T(8,128)(2,1)S(1)} %get-tuple-element.23.low_kept, bf16[2,2,256,512]{3,2,1,0:T(8,128)(2,1)S(1)} %get-tuple-element.20.up_weight, ...), custom_call_target="tpu_custom_call" | custom-call | flops 5000000000 | bytes 4194304 | tf_op jit(solution)/shard_map/end/pallas_call | solution.py:314
  (3 shorter events, 0.1 us)
Async XLA Ops:
  0.0 1.0 %copy-start = (bf16[128,2048]{1,0:T(8,128)(2,1)S(1)}, bf16[128,2048]{1,0:T(8,128)(2,1)}, u32[]{:S(2)}) copy-start(bf16[128,2048]{1,0:T(8,128)(2,1)} %weight_ref.1) | copy-start | bytes 1572868
  1.0 0.7 %copy-start.3 = (f32[32]{0:T(128)S(1)}, f32[32]{0:T(128)}, u32[]{:S(2)}) copy-start(f32[32]{0:T(128)} %param.9) | copy-start | bytes 388
  1.7 3.0 %copy-start.6 = (bf16[64,1,1024]{2,0,1:T(8,128)(2,1)S(1)}, bf16[64,1,1024]{2,0,1:T(8,128)(2,1)}, u32[]{:S(2)}) copy-start(bf16[64,1,1024]{2,0,1:T(8,128)(2,1)} %param.7) | copy-start | bytes 393220
  1.7 20.5 %copy-start.1 = (bf16[27,4096]{1,0:T(8,128)(2,1)S(1)}, bf16[27,4096]{1,0:T(8,128)(2,1)}, u32[]{:S(2)}) copy-start(bf16[27,4096]{1,0:T(8,128)(2,1)} %first_ref.1) | copy-start | bytes 663556
  1.7 20.5 %copy-start.2 = (bf16[27,4096]{1,0:T(8,128)(2,1)S(1)}, bf16[27,4096]{1,0:T(8,128)(2,1)}, u32[]{:S(2)}) copy-start(bf16[27,4096]{1,0:T(8,128)(2,1)} %second_ref.1) | copy-start | bytes 663556
  2.5 10.8 %collective-permute-start.4 = (bf16[1040,128]{1,0:T(8,128)(2,1)S(1)}, bf16[1040,128]{1,0:T(8,128)(2,1)S(1)}, u32[]{:S(2)}, u32[]{:S(2)}) collective-permute-start(bf16[1040,128]{1,0:T(8,128)(2,1)S(1)} %get-tuple-element.17), channel_id=1, source_target_pairs={{0,1},{1,0},{2,3},{3,2},{4,5},{5,4},{6,7},{7,6},{8,9},{9,8},{10,11... | collective-permute-start | bytes 798728 | tf_op jit(solution)/shard_map/ppermute | solution.py:344
  4.7 10.3 %collective-permute-start = (bf16[64,1024]{1,0:T(8,128)(2,1)S(1)}, bf16[64,1024]{1,0:T(8,128)(2,1)S(1)}, u32[]{:S(2)}, u32[]{:S(2)}) collective-permute-start(bf16[64,1024]{1,0:T(8,128)(2,1)S(1)} %bitcast.8), channel_id=1, source_target_pairs={{0,1},{1,0},{2,3},{3,2},{4,5},{5,4},{6,7},{7,6},{8,9},{9,8},{10,11... | collective-permute-start | bytes 393224 | tf_op jit(solution)/shard_map/ppermute | solution.py:342
  13.4 20.8 %collective-permute-start.5 = (bf16[1040,128]{1,0:T(8,128)(2,1)S(1)}, bf16[1040,128]{1,0:T(8,128)(2,1)S(1)}, u32[]{:S(2)}, u32[]{:S(2)}) collective-permute-start(bf16[1040,128]{1,0:T(8,128)(2,1)S(1)} %collective-permute-done.4.up_near_ref), channel_id=1, source_target_pairs={{0,2},{2,0},{4,6},{6,4},{8,10},{10,8},{12,14},{14,12},{16,18},{18,... | collective-permute-start | bytes 798728 | tf_op jit(solution)/shard_map/ppermute | solution.py:349
  15.1 11.9 %collective-permute-start.3 = (bf16[128,1024]{1,0:T(8,128)(2,1)S(1)}, bf16[128,1024]{1,0:T(8,128)(2,1)S(1)}, u32[]{:S(2)}, u32[]{:S(2)}) collective-permute-start(bf16[128,1024]{1,0:T(8,128)(2,1)S(1)} %maximum_select_fusion.own_ref), channel_id=1, source_target_pairs={{2,4},{6,8},{10,12},{14,16},{18,20},{22,24},{26,28},{30,32},{34,36... | collective-permute-start | bytes 786440 | tf_op jit(solution)/shard_map/ppermute | solution.py:346
  22.1 5.0 %collective-permute-start.1 = (bf16[128,1024]{1,0:T(8,128)(2,1)S(1)}, bf16[128,1024]{1,0:T(8,128)(2,1)S(1)}, u32[]{:S(2)}, u32[]{:S(2)}) collective-permute-start(bf16[128,1024]{1,0:T(8,128)(2,1)S(1)} %maximum_select_fusion.own_ref), channel_id=1, source_target_pairs={{0,2},{2,0},{4,6},{6,4},{8,10},{10,8},{12,14},{14,12},{16,18},{18,... | collective-permute-start | bytes 786440 | tf_op jit(solution)/shard_map/ppermute | solution.py:347
  27.0 10.2 %collective-permute-start.6 = (bf16[128,1024]{1,0:T(8,128)(2,1)S(1)}, bf16[128,1024]{1,0:T(8,128)(2,1)S(1)}, u32[]{:S(2)}, u32[]{:S(2)}) collective-permute-start(bf16[128,1024]{1,0:T(8,128)(2,1)S(1)} %collective-permute-done.3.next_ref), channel_id=1, source_target_pairs={{0,2},{2,0},{4,6},{6,4},{8,10},{10,8},{12,14},{14,12},{16,18},{18,... | collective-permute-start | bytes 786440 | tf_op jit(solution)/shard_map/ppermute | solution.py:350
  27.0 14.2 %collective-permute-start.2 = (bf16[128,1024]{1,0:T(8,128)(2,1)S(1)}, bf16[128,1024]{1,0:T(8,128)(2,1)S(1)}, u32[]{:S(2)}, u32[]{:S(2)}) collective-permute-start(bf16[128,1024]{1,0:T(8,128)(2,1)S(1)} %collective-permute-done.1.near_ref), channel_id=1, source_target_pairs={{2,4},{6,8},{10,12},{14,16},{18,20},{22,24},{26,28},{30,32},{34,36... | collective-permute-start | bytes 786440 | tf_op jit(solution)/shard_map/ppermute | solution.py:348
  35.7 1.6 %copy-start.4 = (f32[64]{0:T(128)S(1)}, f32[64]{0:T(128)}, u32[]{:S(2)}) copy-start(f32[64]{0:T(128)} %param.11) | copy-start | bytes 772
  37.3 3.9 %copy-start.5 = (f32[64]{0:T(128)S(1)}, f32[64]{0:T(128)}, u32[]{:S(2)}) copy-start(f32[64]{0:T(128)} %param.13) | copy-start | bytes 772

commit v3 on v2

--- a/solution.py
+++ b/solution.py
@@ -8,6 +8,7 @@
 
 F32 = jnp.float32
 BF16 = jnp.bfloat16
+STEP = 72
 VMEM = pl.BlockSpec(memory_space=pltpu.VMEM)
 SMEM = pl.BlockSpec(memory_space=pltpu.SMEM)
 NT = (((1,), (1,)), ((), ()))
@@ -26,13 +27,15 @@
 
 
 def leaky(value):
-    return jnp.where(value > 0, value, 0.2 * value)
+    return jnp.maximum(value, 0.2 * value)
 
 
 def up_weight_kernel(weight_ref, bias_ref, own_ref, send_ref, rows):
-    rows[...] = weight_ref[...].astype(F32).T
+    turned = weight_ref[...].astype(F32).T
+    for o in range(32):
+        rows[o * STEP : o * STEP + 64, :] = turned[o * 64 : o * 64 + 64]
     for k in range(64):
-        block = rows[pl.ds(k, 32, stride=64), :]
+        block = rows[pl.ds(k, 32, stride=STEP), :]
         own_ref[k // 32, pl.ds((k % 32) * 32, 32), :] = block.astype(BF16)
     bias = jnp.concatenate([bias_ref[...]] * 4, axis=1)
     high = bias.astype(BF16).astype(F32)
@@ -51,7 +54,7 @@
         out_shape=(jax.ShapeDtypeStruct((2, 1040, 128), BF16), jax.ShapeDtypeStruct((1040, 128), BF16)),
         in_specs=[VMEM, VMEM],
         out_specs=(VMEM, VMEM),
-        scratch_shapes=[pltpu.VMEM((2048, 128), F32)],
+        scratch_shapes=[pltpu.VMEM((32 * STEP, 128), F32)],
         compiler_params=params(12),
         cost_estimate=cost(10**9, 2 * 2**20),
         name="prepare_up",
@@ -65,8 +68,8 @@
     def arrange(source, start, count, out_ref):
         for pair in range(count // 2):
             chunk = source[:, pl.ds(start + pair * 128, 128)].astype(F32)
-            spread[pl.ds(2 * pair, 27, stride=64), :] = chunk
-            spread[pl.ds(2 * pair + 1, 27, stride=64), :] = pltpu.roll(chunk, 64, 1)
+            spread[pl.ds(2 * pair, 27, stride=STEP), :] = chunk
+            spread[pl.ds(2 * pair + 1, 27, stride=STEP), :] = pltpu.roll(chunk, 64, 1)
         for eh in range(3):
             for ew in range(3):
                 for zp in range(2):
@@ -76,7 +79,7 @@
                             ed = 2 * zp + zi - zo
                             if 0 <= ed < 3:
                                 ed = ed + odd * (2 - 2 * ed)
-                                start_row = pl.multiple_of((9 * ed + 3 * eh + ew) * 64, 64)
+                                start_row = pl.multiple_of((9 * ed + 3 * eh + ew) * STEP, 8)
                                 tap = spread[pl.ds(start_row, count), :]
                                 halves.append(pltpu.roll(tap, 64, 1) if zi else tap)
                             else:
@@ -95,7 +98,7 @@
         out_shape=(jax.ShapeDtypeStruct((384, 768), BF16), jax.ShapeDtypeStruct((192, 768), BF16)),
         in_specs=[VMEM, VMEM],
         out_specs=(VMEM, VMEM),
-        scratch_shapes=[pltpu.VMEM((27 * 64, 128), F32)],
+        scratch_shapes=[pltpu.VMEM((32 * STEP, 128), F32)],
         compiler_params=params(12),
         cost_estimate=cost(10**9, 2 * 2**20),
         name="prepare_convs",
@@ -254,8 +257,8 @@
     for h in range(32):
         value = leaky(combine(taps, 64, h) + bias)
         for z in range(2):
-            rows_out[pl.ds((z + odd) % 2 * 32 + h, 32, stride=64), :] = value[z * 32 : z * 32 + 32]
-    out_ref[...] = rows_out[...].reshape(32, 2, 32, 128).astype(BF16)
+            rows_out[pl.ds((z + odd) % 2 * 32 + h, 32, stride=STEP), :] = value[z * 32 : z * 32 + 32]
+    out_ref[...] = rows_out[...].reshape(32, STEP, 128)[:, 0:64].reshape(32, 2, 32, 128).astype(BF16)
 
 
 def start(*operands):
@@ -322,7 +325,7 @@
             pltpu.VMEM((4096, 128), F32),
             pltpu.VMEM((384, 4096), F32),
             pltpu.VMEM((128, 4352), BF16),
-            pltpu.VMEM((2048, 128), F32),
+            pltpu.VMEM((32 * STEP, 128), F32),
         ],
         compiler_params=params(28),
         cost_estimate=cost(5 * 10**9, 4 * 2**20),
@@ -337,6 +340,7 @@
     siblings = [(i, i ^ 1) for i in range(devices)]
     across = [(i, i + 1) for i in range(1, devices - 1, 2)]
     across = across + [(j, i) for i, j in across]
+    outward = [(i, i + 2 - i % 2 * 4) for i in range(devices) if 0 <= i + 2 - i % 2 * 4 < devices]
 
     mine = volume.reshape(64, 1024)
     theirs = lax.ppermute(mine, "filt", swap)
@@ -344,8 +348,8 @@
     up_near = lax.ppermute(up_send, "filt", swap)
     own = jnp.where(filt == 0, jnp.concatenate([mine, theirs]), jnp.concatenate([theirs, mine]))
     beyond = lax.ppermute(own, "depth", across)
+    after = lax.ppermute(own, "depth", outward)
     near = lax.ppermute(own, "depth", siblings)
-    after = lax.ppermute(near, "depth", across)
     up_far = lax.ppermute(up_near, "depth", siblings)
     last = lax.ppermute(beyond, "depth", siblings)
     one, two = prepare_convs(first_weight, second_weight)

time: 48.1 us -> 41.5 us (0.86)
  starting transfers between devices: 17.8 us -> 12.6 us
  Pallas kernels: 15.7 us -> 14 us
    ppermute x1, starting transfers between devices: 7.13 us -> 1.92 us  [shards(): after = lax.ppermute(own, 'depth', outward)]
    ppermute x1, waiting for transfers between devices: 0.01 us -> 1.36 us  [shards(): after = lax.ppermute(own, 'depth', outward)]
    ppermute x1, waiting for transfers between devices: 3.23 us -> 2.18 us  [shards(): beyond = lax.ppermute(own, 'depth', across)]
    pallas_call x1, Pallas kernels: 1.6 us -> 0.72 us  [prepare_convs(): pl.pallas_call(conv_weight_kernel, out_shape=(jax.ShapeDtypeStruct((384,...]
  transfers between devices with their start and end apart: 7 -> 7, of which waited for: 3 -> 4; matrix products, arithmetic and copies ran while one was open for 0% -> 0% of each run, Pallas kernels for 18% -> 19%
where the time goes in v3:
time: 41.5 us; the launch traced here: 41 us
  Pallas kernels  14 us (34%)
  starting transfers between devices  12.6 us (30%)
  waiting for transfers between devices  12.5 us (30%)
  local copies, waits for them, and re-layouts  1.72 us (4%)
    ppermute x1, waiting for transfers between devices, shards(): up_near = lax.ppermute(up_send, 'filt', swap)  7.24 us
    ppermute x1, starting transfers between devices, shards(): beyond = lax.ppermute(own, 'depth', across)  6.95 us
    pallas_call x1, Pallas kernels, end(): pl.pallas_call(end_kernel, out_shape=jax.ShapeDtypeStruct((32, 2, 32, 128...  5.98 us
    pallas_call x1, Pallas kernels, late(): pl.pallas_call(late_kernel, out_shape=jax.ShapeDtypeStruct((128, 4352), B...  3.86 us
    ppermute x1, starting transfers between devices, shards(): up_near = lax.ppermute(up_send, 'filt', swap)  2.2 us
    ppermute x1, waiting for transfers between devices, shards(): beyond = lax.ppermute(own, 'depth', across)  2.18 us
    ppermute x1, starting transfers between devices, shards(): after = lax.ppermute(own, 'depth', outward)  1.92 us
    unnamed x14, local copies, waits for them, and re-layouts  1.72 us
  transfers between devices with their start and end apart: 7, of which 4 were waited for; matrix products, arithmetic and copies ran while one was open for 0% of the time, Pallas kernels for 19%

profile of v3, /device:TPU:2, one launch (start us, length us, event | category | flops | bytes accessed | tf_op | source)
XLA Modules:
  0.0 41.0 jit_solution(9204665639804955409)
XLA Ops:
  0.0 0.0 copy-start
  0.0 1.0 %copy-done = bf16[128,2048]{1,0:T(8,128)(2,1)S(1)} copy-done((bf16[128,2048]{1,0:T(8,128)(2,1)S(1)}, bf16[128,2048]{1,0:T(8,128)(2,1)}, u32[]{:S(2)}) %copy-start) | copy-done | bytes 524312
  1.0 0.0 copy-start.3
  1.0 0.7 %copy-done.3 = f32[32]{0:T(128)S(1)} copy-done((f32[32]{0:T(128)S(1)}, f32[32]{0:T(128)}, u32[]{:S(2)}) %copy-start.3) | copy-done | bytes 152
  1.7 0.0 copy-start.6
  1.7 0.4 prepare_up.1
  2.1 2.2 %collective-permute-start.4 = (bf16[1040,128]{1,0:T(8,128)(2,1)S(1)}, bf16[1040,128]{1,0:T(8,128)(2,1)S(1)}, u32[]{:S(2)}, u32[]{:S(2)}) collective-permute-start(bf16[1040,128]{1,0:T(8,128)(2,1)S(1)} %get-tuple-element.17), channel_id=1, source_target_pairs={{0,1},{1,0},{2,3},{3,2},{4,5},{5,4},{6,7},{7,6},{8,9},{9,8},{10,11... | collective-permute-start | bytes 798728 | tf_op jit(solution)/shard_map/ppermute | solution.py:348
  4.3 0.0 copy-done.6
  4.3 1.4 %collective-permute-start = (bf16[64,1024]{1,0:T(8,128)(2,1)S(1)}, bf16[64,1024]{1,0:T(8,128)(2,1)S(1)}, u32[]{:S(2)}, u32[]{:S(2)}) collective-permute-start(bf16[64,1024]{1,0:T(8,128)(2,1)S(1)} %bitcast.8), channel_id=1, source_target_pairs={{0,1},{1,0},{2,3},{3,2},{4,5},{5,4},{6,7},{7,6},{8,9},{9,8},{10,11... | collective-permute-start | bytes 393224 | tf_op jit(solution)/shard_map/ppermute | solution.py:346
  5.7 7.2 %collective-permute-done.4.up_near_ref = bf16[1040,128]{1,0:T(8,128)(2,1)S(1)} collective-permute-done((bf16[1040,128]{1,0:T(8,128)(2,1)S(1)}, bf16[1040,128]{1,0:T(8,128)(2,1)S(1)}, u32[]{:S(2)}, u32[]{:S(2)}) %collective-permute-start.4) | collective-permute-done | bytes 266272 | tf_op jit(solution)/shard_map/ppermute | solution.py:348
  13.0 0.0 collective-permute-start.5
  13.0 1.7 %collective-permute-done = bf16[64,1024]{1,0:T(8,128)(2,1)S(1)} collective-permute-done((bf16[64,1024]{1,0:T(8,128)(2,1)S(1)}, bf16[64,1024]{1,0:T(8,128)(2,1)S(1)}, u32[]{:S(2)}, u32[]{:S(2)}) %collective-permute-start) | collective-permute-done | bytes 131104 | tf_op jit(solution)/shard_map/ppermute | solution.py:346
  14.7 7.0 %collective-permute-start.2 = (bf16[128,1024]{1,0:T(8,128)(2,1)S(1)}, bf16[128,1024]{1,0:T(8,128)(2,1)S(1)}, u32[]{:S(2)}, u32[]{:S(2)}) collective-permute-start(bf16[128,1024]{1,0:T(8,128)(2,1)S(1)} %maximum_select_fusion.own_ref), channel_id=1, source_target_pairs={{2,4},{6,8},{10,12},{14,16},{18,20},{22,24},{26,28},{30,32},{34,36... | collective-permute-start | bytes 786440 | tf_op jit(solution)/shard_map/ppermute | solution.py:350
  21.7 0.1 collective-permute-start.3
  21.8 0.0 copy-done.1
  21.8 0.0 copy-done.2
  21.8 0.7 %prepare_convs.1 = (bf16[384,768]{1,0:T(8,128)(2,1)S(1)}, bf16[192,768]{1,0:T(8,128)(2,1)S(1)}) custom-call(bf16[27,4096]{1,0:T(8,128)(2,1)S(1)} %copy-done.1, bf16[27,4096]{1,0:T(8,128)(2,1)S(1)} %copy-done.2), custom_call_target="tpu_custom_call" | custom-call | flops 1000000000 | bytes 2097152 | tf_op jit(solution)/shard_map/prepare_convs/pallas_call | solution.py:96
  22.5 1.9 %collective-permute-start.1 = (bf16[128,1024]{1,0:T(8,128)(2,1)S(1)}, bf16[128,1024]{1,0:T(8,128)(2,1)S(1)}, u32[]{:S(2)}, u32[]{:S(2)}) collective-permute-start(bf16[128,1024]{1,0:T(8,128)(2,1)S(1)} %maximum_select_fusion.own_ref), channel_id=1, source_target_pairs={{0,4},{4,8},{6,2},{8,12},{10,6},{12,16},{14,10},{16,20},{18,14},{2... | collective-permute-start | bytes 786440 | tf_op jit(solution)/shard_map/ppermute | solution.py:351
  24.4 2.2 %collective-permute-done.2.next_ref = bf16[128,1024]{1,0:T(8,128)(2,1)S(1)} collective-permute-done((bf16[128,1024]{1,0:T(8,128)(2,1)S(1)}, bf16[128,1024]{1,0:T(8,128)(2,1)S(1)}, u32[]{:S(2)}, u32[]{:S(2)}) %collective-permute-start.2) | collective-permute-done | bytes 262176 | tf_op jit(solution)/shard_map/ppermute | solution.py:350
  26.6 0.0 collective-permute-start.6
  26.6 0.0 collective-permute-done.3.near_ref
  26.6 0.0 collective-permute-done.5.up_far_ref
  26.6 1.5 %start.1 = (bf16[2,2,256,512]{3,2,1,0:T(8,128)(2,1)S(1)}, f32[8,128]{1,0:T(8,128)S(1)}, bf16[2,1152,128]{2,1,0:T(8,128)(2,1)S(1)}, bf16[2,2,1024,128]{3,2,1,0:T(8,128)(2,1)S(1)}) custom-call(bf16[128,1024]{1,0:T(8,128)(2,1)S(1)} %maximum_select_fusion.own_ref, bf16[128,1024]{1,0:T(8,128)(2,1)S(1)} %collective-permute-done.3.near_ref, ...), custom_call_target="tpu_custom_call" | custom-call | flops 2000000000 | bytes 4194304 | tf_op jit(solution)/shard_map/start/pallas_call | solution.py:265
  28.1 0.0 copy-start.4
  28.2 1.6 %middle.1 = (bf16[1152,128]{1,0:T(8,128)(2,1)S(1)}, bf16[4352,128]{1,0:T(8,128)(2,1)S(1)}, bf16[2,1024,128]{2,1,0:T(8,128)(2,1)S(1)}) custom-call(bf16[128,1024]{1,0:T(8,128)(2,1)S(1)} %collective-permute-done.2.next_ref, bf16[2,1152,128]{2,1,0:T(8,128)(2,1)S(1)} %get-tuple-element.18.cells, bf16[2,2,1024,128]{3,2,1,0:T(8,128)(2,1)S(1)} %get-tuple-element.19.kept, ...), custom_call_target="tpu_custom_call" | custom-call | flops 2000000000 | bytes 4194304 | tf_op jit(solution)/shard_map/middle/pallas_call | solution.py:282
  29.7 0.0 collective-permute-done.6.last_ref
  29.7 0.0 copy-done.4
  29.7 0.0 copy-start.5
  29.8 3.9 %late.1.hidden_ref = bf16[128,4352]{1,0:T(8,128)(2,1)S(1)} custom-call(bf16[128,1024]{1,0:T(8,128)(2,1)S(1)} %collective-permute-done.6.last_ref, bf16[2,1152,128]{2,1,0:T(8,128)(2,1)S(1)} %get-tuple-element.18.cells, bf16[2,2,1024,128]{3,2,1,0:T(8,128)(2,1)S(1)} %get-tuple-element.19.kept, bf16[2,2,256,512]{3,2,1,0:T(8,128)(2,1)S(1)} %get-tuple-element.20.up_weight, ...), custom_call_target="tpu_custom_call" | custom-call | flops 5000000000 | bytes 4194304 | tf_op jit(solution)/shard_map/late/pallas_call | solution.py:299
  33.6 1.4 %collective-permute-done.1.after_ref = bf16[128,1024]{1,0:T(8,128)(2,1)S(1)} collective-permute-done((bf16[128,1024]{1,0:T(8,128)(2,1)S(1)}, bf16[128,1024]{1,0:T(8,128)(2,1)S(1)}, u32[]{:S(2)}, u32[]{:S(2)}) %collective-permute-start.1) | collective-permute-done | bytes 262176 | tf_op jit(solution)/shard_map/ppermute | solution.py:351
  35.0 0.0 copy-done.5
  35.0 6.0 %end.1 = bf16[32,2,32,128]{3,2,1,0:T(8,128)(2,1)} custom-call(bf16[128,1024]{1,0:T(8,128)(2,1)S(1)} %collective-permute-done.1.after_ref, bf16[1152,128]{1,0:T(8,128)(2,1)S(1)} %get-tuple-element.22.near, bf16[2,1024,128]{2,1,0:T(8,128)(2,1)S(1)} %get-tuple-element.23.low_kept, bf16[2,2,256,512]{3,2,1,0:T(8,128)(2,1)S(1)} %get-tuple-element.20.up_weight, ...), custom_call_target="tpu_custom_call" | custom-call | flops 5000000000 | bytes 4194304 | tf_op jit(solution)/shard_map/end/pallas_call | solution.py:317
  (3 shorter events, 0.1 us)
Async XLA Ops:
  0.0 1.0 %copy-start = (bf16[128,2048]{1,0:T(8,128)(2,1)S(1)}, bf16[128,2048]{1,0:T(8,128)(2,1)}, u32[]{:S(2)}) copy-start(bf16[128,2048]{1,0:T(8,128)(2,1)} %weight_ref.1) | copy-start | bytes 1572868
  1.0 0.7 %copy-start.3 = (f32[32]{0:T(128)S(1)}, f32[32]{0:T(128)}, u32[]{:S(2)}) copy-start(f32[32]{0:T(128)} %param.9) | copy-start | bytes 388
  1.7 2.6 %copy-start.6 = (bf16[64,1,1024]{2,0,1:T(8,128)(2,1)S(1)}, bf16[64,1,1024]{2,0,1:T(8,128)(2,1)}, u32[]{:S(2)}) copy-start(bf16[64,1,1024]{2,0,1:T(8,128)(2,1)} %param.7) | copy-start | bytes 393220
  1.7 20.1 %copy-start.1 = (bf16[27,4096]{1,0:T(8,128)(2,1)S(1)}, bf16[27,4096]{1,0:T(8,128)(2,1)}, u32[]{:S(2)}) copy-start(bf16[27,4096]{1,0:T(8,128)(2,1)} %first_ref.1) | copy-start | bytes 663556
  1.7 20.1 %copy-start.2 = (bf16[27,4096]{1,0:T(8,128)(2,1)S(1)}, bf16[27,4096]{1,0:T(8,128)(2,1)}, u32[]{:S(2)}) copy-start(bf16[27,4096]{1,0:T(8,128)(2,1)} %second_ref.1) | copy-start | bytes 663556
  2.1 10.8 %collective-permute-start.4 = (bf16[1040,128]{1,0:T(8,128)(2,1)S(1)}, bf16[1040,128]{1,0:T(8,128)(2,1)S(1)}, u32[]{:S(2)}, u32[]{:S(2)}) collective-permute-start(bf16[1040,128]{1,0:T(8,128)(2,1)S(1)} %get-tuple-element.17), channel_id=1, source_target_pairs={{0,1},{1,0},{2,3},{3,2},{4,5},{5,4},{6,7},{7,6},{8,9},{9,8},{10,11... | collective-permute-start | bytes 798728 | tf_op jit(solution)/shard_map/ppermute | solution.py:348
  4.3 10.3 %collective-permute-start = (bf16[64,1024]{1,0:T(8,128)(2,1)S(1)}, bf16[64,1024]{1,0:T(8,128)(2,1)S(1)}, u32[]{:S(2)}, u32[]{:S(2)}) collective-permute-start(bf16[64,1024]{1,0:T(8,128)(2,1)S(1)} %bitcast.8), channel_id=1, source_target_pairs={{0,1},{1,0},{2,3},{3,2},{4,5},{5,4},{6,7},{7,6},{8,9},{9,8},{10,11... | collective-permute-start | bytes 393224 | tf_op jit(solution)/shard_map/ppermute | solution.py:346
  13.0 13.7 %collective-permute-start.5 = (bf16[1040,128]{1,0:T(8,128)(2,1)S(1)}, bf16[1040,128]{1,0:T(8,128)(2,1)S(1)}, u32[]{:S(2)}, u32[]{:S(2)}) collective-permute-start(bf16[1040,128]{1,0:T(8,128)(2,1)S(1)} %collective-permute-done.4.up_near_ref), channel_id=1, source_target_pairs={{0,2},{2,0},{4,6},{6,4},{8,10},{10,8},{12,14},{14,12},{16,18},{18,... | collective-permute-start | bytes 798728 | tf_op jit(solution)/shard_map/ppermute | solution.py:353
  14.7 11.9 %collective-permute-start.2 = (bf16[128,1024]{1,0:T(8,128)(2,1)S(1)}, bf16[128,1024]{1,0:T(8,128)(2,1)S(1)}, u32[]{:S(2)}, u32[]{:S(2)}) collective-permute-start(bf16[128,1024]{1,0:T(8,128)(2,1)S(1)} %maximum_select_fusion.own_ref), channel_id=1, source_target_pairs={{2,4},{6,8},{10,12},{14,16},{18,20},{22,24},{26,28},{30,32},{34,36... | collective-permute-start | bytes 786440 | tf_op jit(solution)/shard_map/ppermute | solution.py:350
  21.7 5.0 %collective-permute-start.3 = (bf16[128,1024]{1,0:T(8,128)(2,1)S(1)}, bf16[128,1024]{1,0:T(8,128)(2,1)S(1)}, u32[]{:S(2)}, u32[]{:S(2)}) collective-permute-start(bf16[128,1024]{1,0:T(8,128)(2,1)S(1)} %maximum_select_fusion.own_ref), channel_id=1, source_target_pairs={{0,2},{2,0},{4,6},{6,4},{8,10},{10,8},{12,14},{14,12},{16,18},{18,... | collective-permute-start | bytes 786440 | tf_op jit(solution)/shard_map/ppermute | solution.py:352
  22.5 12.5 %collective-permute-start.1 = (bf16[128,1024]{1,0:T(8,128)(2,1)S(1)}, bf16[128,1024]{1,0:T(8,128)(2,1)S(1)}, u32[]{:S(2)}, u32[]{:S(2)}) collective-permute-start(bf16[128,1024]{1,0:T(8,128)(2,1)S(1)} %maximum_select_fusion.own_ref), channel_id=1, source_target_pairs={{0,4},{4,8},{6,2},{8,12},{10,6},{12,16},{14,10},{16,20},{18,14},{2... | collective-permute-start | bytes 786440 | tf_op jit(solution)/shard_map/ppermute | solution.py:351
  26.6 3.1 %collective-permute-start.6 = (bf16[128,1024]{1,0:T(8,128)(2,1)S(1)}, bf16[128,1024]{1,0:T(8,128)(2,1)S(1)}, u32[]{:S(2)}, u32[]{:S(2)}) collective-permute-start(bf16[128,1024]{1,0:T(8,128)(2,1)S(1)} %collective-permute-done.2.next_ref), channel_id=1, source_target_pairs={{0,2},{2,0},{4,6},{6,4},{8,10},{10,8},{12,14},{14,12},{16,18},{18,... | collective-permute-start | bytes 786440 | tf_op jit(solution)/shard_map/ppermute | solution.py:354
  28.1 1.6 %copy-start.4 = (f32[64]{0:T(128)S(1)}, f32[64]{0:T(128)}, u32[]{:S(2)}) copy-start(f32[64]{0:T(128)} %param.11) | copy-start | bytes 772
  29.7 5.2 %copy-start.5 = (f32[64]{0:T(128)S(1)}, f32[64]{0:T(128)}, u32[]{:S(2)}) copy-start(f32[64]{0:T(128)} %param.13) | copy-start | bytes 772
